TPU v7x, 256 devices: a whole 4x4x8 slice. The times are simulated.
256 devices in a mesh: tile: 32 (over x, z), lev: 8 (over y, core).
Axes of the slice: x: 4, y: 4, z: 8, core: 2. Of those that a mesh axis runs over, the one named last changes fastest.
Arguments:
- ocean_state: bfloat16 [8, 512, 1024, 128], P('lev', 'tile'), may hold values from -6 to 6
- tile_owner: int32 [32, 64], replicated, may hold values from -1 to 1023, as said below
- kernel: bfloat16 [7, 7, 128], replicated, may hold values from -0.875 to 0.875
- bias_dw: float32 [128], replicated, may hold values from -3 to 3
- ln_gain: float32 [128], replicated, may hold values from 0.5 to 2
- ln_bias: float32 [128], replicated, may hold values from -3 to 3
- w_in: bfloat16 [128, 512], replicated, may hold values from -0.5 to 0.5
- b_in: float32 [512], replicated, may hold values from -3 to 3
- w_out: bfloat16 [512, 128], replicated, may hold values from -0.25 to 0.25
- b_out: float32 [128], replicated, may hold values from -3 to 3
- layer_scale: float32 [128], replicated, may hold values from 0.3 to 1.5
- w_vert: bfloat16 [5, 128, 128], replicated, may hold values from -0.25 to 0.25
Outputs:
- updated: bfloat16 [1024, 8, 256, 128], P('tile', None, 'lev')
Inputs may be any that keep to these rules, and one draw needn't show every extreme that they name: `tile_owner`: every value from 0 to 1023 appears exactly once; -1 marks a land tile. Value g names owner g // 32, so every owner receives exactly 32 tiles. No latitude row sends more than 2 tiles to one owner, and in every draw some row sends exactly 2 to some owner.
All inputs are finite; a program needn't handle non-finite values.
Results may differ from a plain program's by a relative error of at most 0.006.
Values may be sent and summed in bfloat16 or wider, within the bound.
No kernel may reach another device: no remote copies, remote signals or barrier semaphores. Data moves between devices by JAX's collectives and lax.ppermute only.
A program may use at most 64 MiB of HBM per device.

v0:
```python
import math

import jax
import jax.numpy as jnp
from jax import lax
from jax.sharding import PartitionSpec as P

CAP = 2


def padded_2(cells, sides, width):
    for axis, dim in sides:
        count = lax.axis_size(axis)
        ends = count - 1
        head = lax.slice_in_dim(cells, 0, width, axis=dim)
        tail = lax.slice_in_dim(cells, cells.shape[dim] - width, cells.shape[dim], axis=dim)
        cells = jnp.concatenate(
            [
                lax.ppermute(tail, axis, [(i, (i + 1) % count) for i in range(ends)]),
                cells,
                lax.ppermute(head, axis, [((i + 1) % count, i) for i in range(ends)]),
            ],
            axis=dim,
        )
    return cells


def depthwise(padded, kernel, bias_dw, rows, cols):
    total = jnp.zeros(padded.shape[:-3] + (rows, cols, padded.shape[-1]), jnp.float32) + bias_dw
    for i in range(7):
        for j in range(7):
            total = total + padded[..., i : i + rows, j : j + cols, :].astype(jnp.float32) * kernel[
                i, j
            ].astype(jnp.float32)
    return total.astype(jnp.bfloat16)


def feed_forward(conv_rows, input_rows, ln_gain, ln_bias, w_in, b_in, w_out, b_out, layer_scale):
    values = conv_rows.astype(jnp.float32)
    centre = jnp.mean(values, axis=-1, keepdims=True)
    spread = jnp.mean((values - centre) ** 2, axis=-1, keepdims=True)
    normed = ((values - centre) / jnp.sqrt(spread + 1e-06) * ln_gain + ln_bias).astype(jnp.bfloat16)
    hidden = jax.nn.gelu(
        jnp.dot(normed, w_in, preferred_element_type=jnp.float32) + b_in, approximate=False
    ).astype(jnp.bfloat16)
    branch = jnp.dot(hidden, w_out, preferred_element_type=jnp.float32) + b_out
    return (input_rows.astype(jnp.float32) + layer_scale * branch).astype(jnp.bfloat16)


def pointwise(tile_conv, tile_input, params):
    out_shape = tile_conv.shape
    channels = out_shape[-1]
    conv_rows = tile_conv.reshape(-1, channels)
    input_rows = tile_input.reshape(-1, channels)
    row_count = conv_rows.shape[0]
    block_rows = math.gcd(row_count, 1024)
    block_count = row_count // block_rows

    def apply_block(blocks):
        return feed_forward(blocks[0], blocks[1], *params)

    result = lax.map(
        apply_block,
        (
            conv_rows.reshape(block_count, block_rows, channels),
            input_rows.reshape(block_count, block_rows, channels),
        ),
    )
    return result.reshape(out_shape)


def vertical(block_mid, w_vert):
    level_count = block_mid.shape[-3]
    widths = [(0, 0)] * (block_mid.ndim - 3) + [(2, 2), (0, 0), (0, 0)]
    level_pad = jnp.pad(block_mid, widths)
    channels = block_mid.shape[-1]
    total = block_mid.astype(jnp.float32)
    for k in range(5):
        taken = level_pad[..., k : k + level_count, :, :].reshape(-1, channels)
        total = total + jnp.dot(taken, w_vert[k], preferred_element_type=jnp.float32).reshape(
            block_mid.shape
        )
    return total.astype(jnp.bfloat16)


def to_columns(block_mid, w_vert):
    return vertical(
        lax.all_to_all(block_mid, "lev", split_axis=2, concat_axis=1, tiled=True), w_vert
    )


def body(
    ocean_state,
    tile_owner,
    kernel,
    bias_dw,
    ln_gain,
    ln_bias,
    w_in,
    b_in,
    w_out,
    b_out,
    layer_scale,
    w_vert,
):
    tile_count = lax.axis_size("tile")
    band_index = lax.axis_index("tile")
    local_levels, tile_side, lon_cells, channels = ocean_state.shape
    lon_tiles = tile_owner.shape[1]
    per_owner = tile_owner.shape[0]
    tile_cells = tile_side * tile_side
    params = (ln_gain, ln_bias, w_in, b_in, w_out, b_out, layer_scale)
    dest_all = jnp.where(tile_owner >= 0, tile_owner // per_owner, -1)
    same_dest = (dest_all[:, :, None] == dest_all[:, None, :]) & (tile_owner[:, :, None] >= 0)
    positions = jnp.arange(lon_tiles, dtype=jnp.int32)
    earlier = positions[None, :] < positions[:, None]
    rank_all = jnp.sum((same_dest & earlier[None]).astype(jnp.int32), axis=2)
    my_owner = lax.dynamic_index_in_dim(tile_owner, band_index, 0, keepdims=False)
    my_dest = lax.dynamic_index_in_dim(dest_all, band_index, 0, keepdims=False)
    my_rank = lax.dynamic_index_in_dim(rank_all, band_index, 0, keepdims=False)
    wet_cols = jnp.repeat(my_owner >= 0, tile_side)
    masked = jnp.where(wet_cols[None, None, :, None], ocean_state, jnp.zeros((), ocean_state.dtype))
    padded = padded_2(masked, (("tile", 1),), 3)
    padded = jnp.concatenate([padded[:, :, -3:], padded, padded[:, :, :3]], axis=2)
    conv_out = depthwise(padded, kernel, bias_dw, tile_side, lon_cells)

    def to_tiles(field_in):
        shaped = field_in.reshape(
            local_levels, tile_side, lon_tiles, tile_side, channels
        ).transpose(2, 0, 1, 3, 4)
        return shaped.reshape(lon_tiles, local_levels, tile_cells, channels)

    slot_ids = jnp.arange(tile_count * CAP, dtype=jnp.int32)
    match_table = (my_dest[None, :] == (slot_ids // CAP)[:, None]) & (
        my_rank[None, :] == (slot_ids % CAP)[:, None]
    )
    pick_index = jnp.argmax(match_table.astype(jnp.int32), axis=1)
    present = jnp.any(match_table, axis=1)
    owner_flat = tile_owner.reshape(-1)
    target = band_index * per_owner + jnp.arange(per_owner, dtype=jnp.int32)
    hit_table = (owner_flat[None, :] == target[:, None]).astype(jnp.int32)
    src_flat = jnp.argmax(hit_table, axis=1)
    src_band = src_flat // lon_tiles
    src_rank = rank_all.reshape(-1)[src_flat]
    recv_index = src_band * CAP + src_rank
    band_mid = pointwise(to_tiles(conv_out), to_tiles(masked), params)
    selected = band_mid[pick_index]
    selected = jnp.where(present[:, None, None, None], selected, jnp.zeros((), selected.dtype))
    received = lax.all_to_all(
        selected.reshape(tile_count, CAP, local_levels, tile_cells, channels),
        "tile",
        split_axis=0,
        concat_axis=0,
        tiled=True,
    )
    block_mid = received.reshape(tile_count * CAP, received.shape[2], received.shape[3], channels)[
        recv_index
    ]
    return to_columns(block_mid, w_vert)


def solution(mesh):
    return jax.shard_map(
        body,
        mesh=mesh,
        in_specs=(
            P("lev", "tile", None, None),
            P(),
            P(),
            P(),
            P(),
            P(),
            P(),
            P(),
            P(),
            P(),
            P(),
            P(),
        ),
        out_specs=P("tile", None, "lev", None),
        check_vma=False,
    )
```

profile of v0, /device:TPU:1, one launch (start us, length us, event | category | flops | bytes accessed | tf_op | source)
XLA Modules:
  0.0 441.6 jit_solution(5957688788820809960)
XLA Ops:
  0.9 2.7 broadcast_select_fusion
  5.7 4.4 %collective-permute-start = (bf16[1,3,1024,128]{3,2,1,0:T(8,128)(2,1)S(1)}, bf16[1,3,1024,128]{3,2,1,0:T(8,128)(2,1)S(1)}, u32[]{:S(2)}, u32[]{:S(2)}) collective-permute-start(bf16[1,3,1024,128]{3,2,1,0:T(8,128)(2,1)S(1)} %get-tuple-element.91), channel_id=1, source_target_pairs={{0,8},{8,16},{16,24},{24,32},{32,40},{40,48},{48,56},{56,64},{64,7... | collective-permute-start | bytes 2359304 | tf_op jit(solution)/shard_map/ppermute | solution.py:19
  13.8 5.3 %copy.24 = bf16[1,16,64,16,128]{4,3,1,2,0:T(8,128)(2,1)} copy(bf16[1,16,64,16,128]{4,3,2,1,0:T(8,128)(2,1)} %bitcast.245) | data formatting | bytes 8388608 | tf_op jit(solution)/shard_map/reshape | solution.py:128
  19.4 6.9 %collective-permute-done = bf16[1,3,1024,128]{3,2,1,0:T(8,128)(2,1)S(1)} collective-permute-done((bf16[1,3,1024,128]{3,2,1,0:T(8,128)(2,1)S(1)}, bf16[1,3,1024,128]{3,2,1,0:T(8,128)(2,1)S(1)}, u32[]{:S(2)}, u32[]{:S(2)}) %collective-permute-start) | collective-permute-done | bytes 786464 | tf_op jit(solution)/shard_map/ppermute | solution.py:19
  26.3 4.1 collective-permute-done.1
  30.4 18.6 %fusion.100 = (bf16[1,22,1027,128]{3,2,1,0:T(8,128)(2,1)S(1)}, bf16[1,22,1027,128]{3,2,1,0:T(8,128)(2,1)S(1)}) fusion(bf16[1,3,1024,128]{3,2,1,0:T(8,128)(2,1)S(1)} %collective-permute-done.1, bf16[1,16,1024,128]{3,2,1,0:T(8,128)(2,1)} %copy-done, bf16[1,3,1024,128]{3,2,1,0:T(8,128)(2,1)S(1)} %collective-permute-done), kind=kLoop, calls=%fused_computation.116 | loop fusion | flops 69408768 | bytes 17335296 | tf_op jit(solution)/shard_map/concatenate | solution.py:124
  49.0 78.4 %add_convert_fusion = bf16[1,16,1024,128]{3,2,1,0:T(8,128)(2,1)S(1)} fusion(bf16[1,16,1024,128]{3,2,1,0:T(8,128)(2,1)S(1)} %copy-done.1, bf16[1,3,1024,128]{3,2,1,0:T(8,128)(2,1)S(1)} %collective-permute-done.1, bf16[1,3,1024,128]{3,2,1,0:T(8,128)(2,1)S(1)} %collective-permute-done, bf16[1,22,1027,128]{3,2,1,0:T(8,128)(2,1)S(1)} %get-tuple-element.90, ...), kind=kLoop, calls=%fused_computation.107 | loop fusion | flops 322961408 | bytes 186147840 | tf_op jit(solution)/shard_map/convert_element_type | solution.py:35
  127.5 3.2 copy.25
  130.8 150.7 %while.10 = (s32[]{:T(128)}, bf16[16,1024,128]{2,1,0:T(8,128)(2,1)}, bf16[16,1024,128]{2,1,0:T(8,128)(2,1)}, f32[128]{0:T(128)S(1)}, bf16[16,1024,128]{2,1,0:T(8...) while((s32[]{:T(128)}, ...), condition=%wide.region_5.6_spmd, body=%wide.region_2.5_spmd.sunk | while | flops 305267712 | bytes 1614973 | solution.py:62
  133.4 7.0 %fusion.142 = bf16[16,1024,128]{2,1,0:T(8,128)(2,1)} fusion(bf16[16,1024,128]{2,1,0:T(8,128)(2,1)} %get-tuple-element.226, s32[]{:T(128)} %get-tuple-element.225, bf16[512,128]{1,0:T(8,128)(2,1)S(1)} %get-tuple-element.246, bf16[128,512]{1,0:T(8,128)(2,1)S(1)} %get-tuple-element.244, f32[512]{0:T(512)S(1)} %get-tuple-element.245, ...), kind=kOutput, calls=%fused_computation.28.clone.1 | convolution fusion | flops 304480256 | bytes 1061888 | tf_op jit(solution)/shard_map/while/body/eval_jaxpr/dot_general | solution.py:46
  142.8 7.0 %fusion.142 = bf16[16,1024,128]{2,1,0:T(8,128)(2,1)} fusion(bf16[16,1024,128]{2,1,0:T(8,128)(2,1)} %get-tuple-element.226, s32[]{:T(128)} %get-tuple-element.225, bf16[512,128]{1,0:T(8,128)(2,1)S(1)} %get-tuple-element.246, bf16[128,512]{1,0:T(8,128)(2,1)S(1)} %get-tuple-element.244, f32[512]{0:T(512)S(1)} %get-tuple-element.245, ...), kind=kOutput, calls=%fused_computation.28.clone.1 | convolution fusion | flops 304480256 | bytes 1061888 | tf_op jit(solution)/shard_map/while/body/eval_jaxpr/dot_general | solution.py:46
  152.2 7.0 %fusion.142 = bf16[16,1024,128]{2,1,0:T(8,128)(2,1)} fusion(bf16[16,1024,128]{2,1,0:T(8,128)(2,1)} %get-tuple-element.226, s32[]{:T(128)} %get-tuple-element.225, bf16[512,128]{1,0:T(8,128)(2,1)S(1)} %get-tuple-element.246, bf16[128,512]{1,0:T(8,128)(2,1)S(1)} %get-tuple-element.244, f32[512]{0:T(512)S(1)} %get-tuple-element.245, ...), kind=kOutput, calls=%fused_computation.28.clone.1 | convolution fusion | flops 304480256 | bytes 1061888 | tf_op jit(solution)/shard_map/while/body/eval_jaxpr/dot_general | solution.py:46
  161.6 7.0 %fusion.142 = bf16[16,1024,128]{2,1,0:T(8,128)(2,1)} fusion(bf16[16,1024,128]{2,1,0:T(8,128)(2,1)} %get-tuple-element.226, s32[]{:T(128)} %get-tuple-element.225, bf16[512,128]{1,0:T(8,128)(2,1)S(1)} %get-tuple-element.246, bf16[128,512]{1,0:T(8,128)(2,1)S(1)} %get-tuple-element.244, f32[512]{0:T(512)S(1)} %get-tuple-element.245, ...), kind=kOutput, calls=%fused_computation.28.clone.1 | convolution fusion | flops 304480256 | bytes 1061888 | tf_op jit(solution)/shard_map/while/body/eval_jaxpr/dot_general | solution.py:46
  171.0 7.0 %fusion.142 = bf16[16,1024,128]{2,1,0:T(8,128)(2,1)} fusion(bf16[16,1024,128]{2,1,0:T(8,128)(2,1)} %get-tuple-element.226, s32[]{:T(128)} %get-tuple-element.225, bf16[512,128]{1,0:T(8,128)(2,1)S(1)} %get-tuple-element.246, bf16[128,512]{1,0:T(8,128)(2,1)S(1)} %get-tuple-element.244, f32[512]{0:T(512)S(1)} %get-tuple-element.245, ...), kind=kOutput, calls=%fused_computation.28.clone.1 | convolution fusion | flops 304480256 | bytes 1061888 | tf_op jit(solution)/shard_map/while/body/eval_jaxpr/dot_general | solution.py:46
  180.4 7.0 %fusion.142 = bf16[16,1024,128]{2,1,0:T(8,128)(2,1)} fusion(bf16[16,1024,128]{2,1,0:T(8,128)(2,1)} %get-tuple-element.226, s32[]{:T(128)} %get-tuple-element.225, bf16[512,128]{1,0:T(8,128)(2,1)S(1)} %get-tuple-element.246, bf16[128,512]{1,0:T(8,128)(2,1)S(1)} %get-tuple-element.244, f32[512]{0:T(512)S(1)} %get-tuple-element.245, ...), kind=kOutput, calls=%fused_computation.28.clone.1 | convolution fusion | flops 304480256 | bytes 1061888 | tf_op jit(solution)/shard_map/while/body/eval_jaxpr/dot_general | solution.py:46
  189.9 7.0 %fusion.142 = bf16[16,1024,128]{2,1,0:T(8,128)(2,1)} fusion(bf16[16,1024,128]{2,1,0:T(8,128)(2,1)} %get-tuple-element.226, s32[]{:T(128)} %get-tuple-element.225, bf16[512,128]{1,0:T(8,128)(2,1)S(1)} %get-tuple-element.246, bf16[128,512]{1,0:T(8,128)(2,1)S(1)} %get-tuple-element.244, f32[512]{0:T(512)S(1)} %get-tuple-element.245, ...), kind=kOutput, calls=%fused_computation.28.clone.1 | convolution fusion | flops 304480256 | bytes 1061888 | tf_op jit(solution)/shard_map/while/body/eval_jaxpr/dot_general | solution.py:46
  199.3 7.0 %fusion.142 = bf16[16,1024,128]{2,1,0:T(8,128)(2,1)} fusion(bf16[16,1024,128]{2,1,0:T(8,128)(2,1)} %get-tuple-element.226, s32[]{:T(128)} %get-tuple-element.225, bf16[512,128]{1,0:T(8,128)(2,1)S(1)} %get-tuple-element.246, bf16[128,512]{1,0:T(8,128)(2,1)S(1)} %get-tuple-element.244, f32[512]{0:T(512)S(1)} %get-tuple-element.245, ...), kind=kOutput, calls=%fused_computation.28.clone.1 | convolution fusion | flops 304480256 | bytes 1061888 | tf_op jit(solution)/shard_map/while/body/eval_jaxpr/dot_general | solution.py:46
  208.7 7.0 %fusion.142 = bf16[16,1024,128]{2,1,0:T(8,128)(2,1)} fusion(bf16[16,1024,128]{2,1,0:T(8,128)(2,1)} %get-tuple-element.226, s32[]{:T(128)} %get-tuple-element.225, bf16[512,128]{1,0:T(8,128)(2,1)S(1)} %get-tuple-element.246, bf16[128,512]{1,0:T(8,128)(2,1)S(1)} %get-tuple-element.244, f32[512]{0:T(512)S(1)} %get-tuple-element.245, ...), kind=kOutput, calls=%fused_computation.28.clone.1 | convolution fusion | flops 304480256 | bytes 1061888 | tf_op jit(solution)/shard_map/while/body/eval_jaxpr/dot_general | solution.py:46
  218.1 7.0 %fusion.142 = bf16[16,1024,128]{2,1,0:T(8,128)(2,1)} fusion(bf16[16,1024,128]{2,1,0:T(8,128)(2,1)} %get-tuple-element.226, s32[]{:T(128)} %get-tuple-element.225, bf16[512,128]{1,0:T(8,128)(2,1)S(1)} %get-tuple-element.246, bf16[128,512]{1,0:T(8,128)(2,1)S(1)} %get-tuple-element.244, f32[512]{0:T(512)S(1)} %get-tuple-element.245, ...), kind=kOutput, calls=%fused_computation.28.clone.1 | convolution fusion | flops 304480256 | bytes 1061888 | tf_op jit(solution)/shard_map/while/body/eval_jaxpr/dot_general | solution.py:46
  227.5 7.0 %fusion.142 = bf16[16,1024,128]{2,1,0:T(8,128)(2,1)} fusion(bf16[16,1024,128]{2,1,0:T(8,128)(2,1)} %get-tuple-element.226, s32[]{:T(128)} %get-tuple-element.225, bf16[512,128]{1,0:T(8,128)(2,1)S(1)} %get-tuple-element.246, bf16[128,512]{1,0:T(8,128)(2,1)S(1)} %get-tuple-element.244, f32[512]{0:T(512)S(1)} %get-tuple-element.245, ...), kind=kOutput, calls=%fused_computation.28.clone.1 | convolution fusion | flops 304480256 | bytes 1061888 | tf_op jit(solution)/shard_map/while/body/eval_jaxpr/dot_general | solution.py:46
  236.9 7.0 %fusion.142 = bf16[16,1024,128]{2,1,0:T(8,128)(2,1)} fusion(bf16[16,1024,128]{2,1,0:T(8,128)(2,1)} %get-tuple-element.226, s32[]{:T(128)} %get-tuple-element.225, bf16[512,128]{1,0:T(8,128)(2,1)S(1)} %get-tuple-element.246, bf16[128,512]{1,0:T(8,128)(2,1)S(1)} %get-tuple-element.244, f32[512]{0:T(512)S(1)} %get-tuple-element.245, ...), kind=kOutput, calls=%fused_computation.28.clone.1 | convolution fusion | flops 304480256 | bytes 1061888 | tf_op jit(solution)/shard_map/while/body/eval_jaxpr/dot_general | solution.py:46
  246.3 7.0 %fusion.142 = bf16[16,1024,128]{2,1,0:T(8,128)(2,1)} fusion(bf16[16,1024,128]{2,1,0:T(8,128)(2,1)} %get-tuple-element.226, s32[]{:T(128)} %get-tuple-element.225, bf16[512,128]{1,0:T(8,128)(2,1)S(1)} %get-tuple-element.246, bf16[128,512]{1,0:T(8,128)(2,1)S(1)} %get-tuple-element.244, f32[512]{0:T(512)S(1)} %get-tuple-element.245, ...), kind=kOutput, calls=%fused_computation.28.clone.1 | convolution fusion | flops 304480256 | bytes 1061888 | tf_op jit(solution)/shard_map/while/body/eval_jaxpr/dot_general | solution.py:46
  255.7 6.9 %fusion.142 = bf16[16,1024,128]{2,1,0:T(8,128)(2,1)} fusion(bf16[16,1024,128]{2,1,0:T(8,128)(2,1)} %get-tuple-element.226, s32[]{:T(128)} %get-tuple-element.225, bf16[512,128]{1,0:T(8,128)(2,1)S(1)} %get-tuple-element.246, bf16[128,512]{1,0:T(8,128)(2,1)S(1)} %get-tuple-element.244, f32[512]{0:T(512)S(1)} %get-tuple-element.245, ...), kind=kOutput, calls=%fused_computation.28.clone.1 | convolution fusion | flops 304480256 | bytes 1061888 | tf_op jit(solution)/shard_map/while/body/eval_jaxpr/dot_general | solution.py:46
  265.1 7.0 %fusion.142 = bf16[16,1024,128]{2,1,0:T(8,128)(2,1)} fusion(bf16[16,1024,128]{2,1,0:T(8,128)(2,1)} %get-tuple-element.226, s32[]{:T(128)} %get-tuple-element.225, bf16[512,128]{1,0:T(8,128)(2,1)S(1)} %get-tuple-element.246, bf16[128,512]{1,0:T(8,128)(2,1)S(1)} %get-tuple-element.244, f32[512]{0:T(512)S(1)} %get-tuple-element.245, ...), kind=kOutput, calls=%fused_computation.28.clone.1 | convolution fusion | flops 304480256 | bytes 1061888 | tf_op jit(solution)/shard_map/while/body/eval_jaxpr/dot_general | solution.py:46
  274.5 7.0 %fusion.142 = bf16[16,1024,128]{2,1,0:T(8,128)(2,1)} fusion(bf16[16,1024,128]{2,1,0:T(8,128)(2,1)} %get-tuple-element.226, s32[]{:T(128)} %get-tuple-element.225, bf16[512,128]{1,0:T(8,128)(2,1)S(1)} %get-tuple-element.246, bf16[128,512]{1,0:T(8,128)(2,1)S(1)} %get-tuple-element.244, f32[512]{0:T(512)S(1)} %get-tuple-element.245, ...), kind=kOutput, calls=%fused_computation.28.clone.1 | convolution fusion | flops 304480256 | bytes 1061888 | tf_op jit(solution)/shard_map/while/body/eval_jaxpr/dot_general | solution.py:46
  281.5 5.2 %gather_fusion = bf16[64,256,128]{2,1,0:T(8,128)(2,1)} fusion(bf16[64,256,128]{2,1,0:T(8,128)(2,1)} %bitcast.256, s32[1024]{0:T(1024)S(1)} %pad_clamp_fusion.2), kind=kCustom, calls=%fused_computation | custom fusion | bytes 8388864 | tf_op jit(solution)/shard_map/gather | solution.py:147
  286.7 4.5 %broadcast_select_fusion.1 = bf16[32,2,1,256,128]{4,3,1,2,0:T(8,128)(2,1)} fusion(bf16[32,2,1,256,128]{4,3,1,2,0:T(8,128)(2,1)} %bitcast.252, pred[32,2]{1,0:T(8,128)(4,1)S(1)} %broadcast_in_dim.39), kind=kLoop, calls=%fused_computation.130 | loop fusion | flops 2097152 | bytes 8388672 | tf_op jit(solution)/shard_map/jit(_where)/select_n | solution.py:148
  291.2 10.7 %all-to-all-start = ((bf16[32,2,1,256,128]{4,3,1,2,0:T(8,128)(2,1)}), bf16[32,2,1,256,128]{4,3,1,2,0:T(8,128)(2,1)}, u32[]{:S(2)}, u32[]{:S(2)}) async-start(bf16[32,2,1,256,128]{4,3,1,2,0:T(8,128)(2,1)} %broadcast_select_fusion.1), calls=%async_computation | async-start | bytes 8388608 | tf_op jit(solution)/shard_map/all_to_all | solution.py:149
  303.5 93.9 %all-to-all-done = bf16[32,2,1,256,128]{4,3,1,2,0:T(8,128)(2,1)} async-done(((bf16[32,2,1,256,128]{4,3,1,2,0:T(8,128)(2,1)}), bf16[32,2,1,256,128]{4,3,1,2,0:T(8,128)(2,1)}, u32[]{:S(2)}, u32[]{:S(2)}) %all-to-all-start) | async-done | bytes 4194336 | tf_op jit(solution)/shard_map/all_to_all | solution.py:149
  397.4 3.1 gather_fusion.2
  401.9 33.5 %all_to_all.17 = bf16[32,1,256,128]{3,0,1,2:T(8,128)(2,1)S(1)} all-to-all(bf16[32,1,256,128]{3,0,1,2:T(8,128)(2,1)S(1)} %copy.26), channel_id=1, replica_groups=mesh['tile'=32,'lev'=8] {'lev'}, dimensions={2} | all-to-all | bytes 4194304 | tf_op jit(solution)/shard_map/all_to_all | solution.py:88
  438.9 2.7 add_convert_fusion.1
  (125 shorter events, 52.0 us)
Async XLA Ops:
  0.9 10.5 %copy-start.3 = (s32[32,64]{1,0:T(8,128)S(1)}, s32[32,64]{1,0:T(8,128)}, u32[]{:S(2)}) copy-start(s32[32,64]{1,0:T(8,128)} %param.15) | copy-start | bytes 24580
  3.6 2.0 copy-start
  5.7 13.6 %copy-start.4 = (bf16[7,7,128]{2,1,0:T(8,128)(2,1)S(1)}, bf16[7,7,128]{2,1,0:T(8,128)(2,1)}, u32[]{:S(2)}) copy-start(bf16[7,7,128]{2,1,0:T(8,128)(2,1)} %param.16) | copy-start | bytes 37636
  5.7 20.6 %collective-permute-start = (bf16[1,3,1024,128]{3,2,1,0:T(8,128)(2,1)S(1)}, bf16[1,3,1024,128]{3,2,1,0:T(8,128)(2,1)S(1)}, u32[]{:S(2)}, u32[]{:S(2)}) collective-permute-start(bf16[1,3,1024,128]{3,2,1,0:T(8,128)(2,1)S(1)} %get-tuple-element.91), channel_id=1, source_target_pairs={{0,8},{8,16},{16,24},{24,32},{32,40},{40,48},{48,56},{56,64},{64,7... | collective-permute-start | bytes 2359304 | tf_op jit(solution)/shard_map/ppermute | solution.py:19
  10.1 20.3 %collective-permute-start.1 = (bf16[1,3,1024,128]{3,2,1,0:T(8,128)(2,1)S(1)}, bf16[1,3,1024,128]{3,2,1,0:T(8,128)(2,1)S(1)}, u32[]{:S(2)}, u32[]{:S(2)}) collective-permute-start(bf16[1,3,1024,128]{3,2,1,0:T(8,128)(2,1)S(1)} %get-tuple-element.92), channel_id=1, source_target_pairs={{8,0},{16,8},{24,16},{32,24},{40,32},{48,40},{56,48},{64,56},{72,6... | collective-permute-start | bytes 2359304 | tf_op jit(solution)/shard_map/ppermute | solution.py:21
  19.3 29.7 %copy-start.1 = (bf16[1,16,1024,128]{3,2,1,0:T(8,128)(2,1)S(1)}, bf16[1,16,1024,128]{3,2,1,0:T(8,128)(2,1)}, u32[]{:S(2)}) copy-start(bf16[1,16,1024,128]{3,2,1,0:T(8,128)(2,1)} %copy-done) | copy-start | bytes 12582916
  19.3 29.7 %copy-start.5 = (f32[128]{0:T(128)S(1)}, f32[128]{0:T(128)}, u32[]{:S(2)}) copy-start(f32[128]{0:T(128)} %param.17) | copy-start | bytes 1540
  127.4 3.3 copy-start.6
  127.5 3.3 copy-start.7
  127.5 3.3 copy-start.8
  127.5 3.2 copy-start.9
  127.5 3.2 copy-start.10
  127.5 3.2 copy-start.11
  127.5 3.2 copy-start.12
  291.2 106.2 %all-to-all-start = ((bf16[32,2,1,256,128]{4,3,1,2,0:T(8,128)(2,1)}), bf16[32,2,1,256,128]{4,3,1,2,0:T(8,128)(2,1)}, u32[]{:S(2)}, u32[]{:S(2)}) async-start(bf16[32,2,1,256,128]{4,3,1,2,0:T(8,128)(2,1)} %broadcast_select_fusion.1), calls=%async_computation | async-start | bytes 8388608 | tf_op jit(solution)/shard_map/all_to_all | solution.py:149
  401.9 34.3 %copy-start.2 = (bf16[5,128,128]{2,1,0:T(8,128)(2,1)S(1)}, bf16[5,128,128]{2,1,0:T(8,128)(2,1)}, u32[]{:S(2)}) copy-start(bf16[5,128,128]{2,1,0:T(8,128)(2,1)} %param.25) | copy-start | bytes 491524
where the time goes:
time: 443 us; the launch traced here: 442 us
  other arithmetic  147 us (33%)
  matrix products  117 us (26%)
  waiting for transfers between devices  105 us (24%)
  blocking collectives  33.5 us (8%)
  local copies, waits for them, and re-layouts  22.3 us (5%)
  starting transfers between devices  16.4 us (4%)
    dot_general x16, matrix products, feed_forward(): branch = jnp.dot(hidden, w_out, preferred_element_type=jnp.float32) + b_out  111 us
    all_to_all x1, waiting for transfers between devices, body(): lax.all_to_all(selected.reshape(tile_count, CAP, local_levels, tile_cells...  93.9 us
    convert_element_type x1, other arithmetic, depthwise(): return total.astype(jnp.bfloat16)  78.4 us
    all_to_all x1, blocking collectives, to_columns(): lax.all_to_all(block_mid, 'lev', split_axis=2, concat_axis=1, tiled=True)  33.5 us
    reduce_sum x16, other arithmetic, feed_forward(): spread = jnp.mean((values - centre) ** 2, axis=-1, keepdims=True)  21 us
    concatenate x1, other arithmetic, body(): jnp.concatenate([padded[:, :, -3:], padded, padded[:, :, :3]], axis=2)  18.6 us
    reduce_sum x16, other arithmetic, feed_forward(): centre = jnp.mean(values, axis=-1, keepdims=True)  17.5 us
    all_to_all x1, starting transfers between devices, body(): lax.all_to_all(selected.reshape(tile_count, CAP, local_levels, tile_cells...  10.7 us
  transfers between devices with their start and end apart: 3, of which 3 were waited for; matrix products, arithmetic and copies ran while one was open for 2% of the time, Pallas kernels for 0%

commit v1 on v0

v1 whole, which is shorter than its diff:
```python
import functools

import jax
import jax.numpy as jnp
from jax import lax
from jax.experimental import pallas as pl
from jax.experimental.pallas import tpu as pltpu
from jax.sharding import PartitionSpec as P

CAP = 2
TS = 16
C = 128
F32 = jnp.float32
BF16 = jnp.bfloat16
SLOTS = 2


def list_wet(owner_ref, band, seen, cols, slots):
    lon = owner_ref.shape[1]
    per_owner = owner_ref.shape[0]

    def clear(o, _):
        seen[o] = 0
        return 0

    lax.fori_loop(0, per_owner, clear, 0)

    def scan(c, count):
        g = owner_ref[band, c]
        wet = g >= 0
        dest = lax.shift_right_logical(jnp.maximum(g, 0), per_owner.bit_length() - 1)
        rank = seen[dest]
        cols[count] = c
        slots[count] = dest * CAP + rank
        seen[dest] = rank + wet.astype(jnp.int32)
        return count + wet.astype(jnp.int32)

    return lax.fori_loop(0, lon, scan, 0)


def conv_rows(pad_ref, first, taps, bias, rows):
    total = [[bias, bias] for _ in range(rows)]
    for j in range(7):
        ks = [taps[i * 7 + j] for i in range(7)]
        for yi in range(rows + 6):
            for h in range(2):
                v = pad_ref[first + yi, pl.ds(5 + j + 8 * h, 8), :]
                for i in range(7):
                    y = yi - i
                    if 0 <= y < rows:
                        total[y][h] = total[y][h] + v * ks[i]
    return jnp.concatenate([t for pair in total for t in pair], axis=0)


def pointwise(conv, inp, gain, shift, w_in, b_in, w_out, b_out, scale):
    values = conv.astype(F32)
    centre = jnp.mean(values, axis=-1, keepdims=True)
    dev = values - centre
    spread = jnp.mean(dev * dev, axis=-1, keepdims=True)
    normed = (dev * lax.rsqrt(spread + 1e-06) * gain + shift).astype(BF16)
    h = jnp.dot(normed, w_in, preferred_element_type=F32) + b_in
    half = 0.5 * h
    hidden = (half + half * lax.erf(h * 0.7071067811865476)).astype(BF16)
    branch = jnp.dot(hidden, w_out, preferred_element_type=F32) + b_out
    return (inp.astype(F32) + scale * branch).astype(BF16)


def fill(pad_ref, first, src, row0, rows, t, lon, wet):
    left = lax.rem(t + lon - 1, lon)
    right = lax.rem(t + 1, lon)

    def tile(col):
        return src[pl.ds(row0, rows), pl.ds(pl.multiple_of(col * TS, TS), TS), :].astype(F32)

    keep_l, keep_c, keep_r = wet
    zero = jnp.zeros((), F32)
    centre = tile(t)
    if keep_c is not None:
        centre = jnp.where(keep_c, centre, zero)
    pad_ref[pl.ds(first, rows), pl.ds(0, 8), :] = jnp.where(keep_l, tile(left)[:, 8:, :], zero)
    pad_ref[pl.ds(first, rows), pl.ds(8, 16), :] = centre
    pad_ref[pl.ds(first, rows), pl.ds(24, 8), :] = jnp.where(keep_r, tile(right)[:, :8, :], zero)


def neighbours(owner_ref, band, t, lon):
    left = lax.rem(t + lon - 1, lon)
    right = lax.rem(t + 1, lon)
    return (owner_ref[band, left] >= 0, owner_ref[band, t] >= 0, owner_ref[band, right] >= 0)


def block_kernel(inner, *refs):
    if inner:
        (owner_ref, x_ref, taps_in, bias_ref, gain, shift, w_in, b_in, w_out, b_out, scale,
         send, pad, taps, convbuf, stage, seen, cols, slots, sem) = refs
        top = bottom = None
    else:
        (owner_ref, x_ref, top, bottom, taps_in, bias_ref, gain, shift, w_in, b_in, w_out, b_out,
         scale, _, send, pad, taps, convbuf, stage, seen, cols, slots, sem) = refs
    lon = owner_ref.shape[1]
    bands = owner_ref.shape[0]
    band = lax.axis_index("tile")
    count = list_wet(owner_ref, band, seen, cols, slots)
    for i in range(7):
        for j in range(7):
            taps[i * 7 + j] = jnp.broadcast_to(taps_in[i, pl.ds(j, 1), :].astype(F32), (8, C))
    convbuf[...] = jnp.zeros_like(convbuf)
    cells = convbuf.shape[0]

    def copies(index, b):
        slot = slots[index]
        dest, rank = lax.shift_right_logical(slot, 1), lax.bitwise_and(slot, 1)

        def piece(q, lo, n, lev, nlev, off, width):
            if nlev > 1:
                src = stage.at[b, pl.ds(lo, n)].reshape(nlev, width, C)
                dst = send.at[dest, pl.ds(lev, nlev), rank]
            else:
                src = stage.at[b, pl.ds(lo, n)]
                dst = send.at[dest, lev, rank, pl.ds(off, width)]
            return pltpu.make_async_copy(src, dst, sem.at[b, q])

        if inner:
            return [piece(0, 0, 16, 1, 1, 16, 16), piece(1, 16, 128, 2, 4, 0, 32),
                    piece(2, 144, 16, 6, 1, 0, 16)]
        return [piece(0, 0, 32, 0, 1, 0, 32), piece(1, 32, 16, 1, 1, 0, 16),
                piece(2, 48, 16, 6, 1, 16, 16), piece(3, 64, 32, 7, 1, 0, 32)]

    def step(n, _):
        now = jnp.minimum(n, count - 1)
        before = jnp.maximum(n - 1, 0)
        b = lax.rem(before, SLOTS)

        @pl.when(n > SLOTS)
        def _():
            for cp in copies(before - SLOTS, b):
                cp.wait()

        t, tb = cols[now], cols[before]
        own = neighbours(owner_ref, band, t, lon)
        old = convbuf[...]
        column = pl.ds(pl.multiple_of(tb * TS, TS), TS)
        if inner:
            inp = x_ref[pl.ds(3, 10), column, :].reshape(cells, C)
        else:
            inp = jnp.concatenate(
                [x_ref[pl.ds(0, 3), column, :].reshape(cells // 2, C),
                 x_ref[pl.ds(13, 3), column, :].reshape(cells // 2, C)], axis=0)
        stage[b] = pointwise(old, inp, gain[...], shift[...], w_in[...], b_in[...], w_out[...],
                             b_out[...], scale[...])
        bias = jnp.broadcast_to(bias_ref[...], (8, C))
        keep = (own[0], None, own[2])
        if inner:
            fill(pad, 0, x_ref, 0, 16, t, lon, keep)
            convbuf[...] = conv_rows(pad, 0, taps, bias, 10).astype(BF16)
        else:
            up = neighbours(owner_ref, jnp.maximum(band - 1, 0), t, lon)
            down = neighbours(owner_ref, jnp.minimum(band + 1, bands - 1), t, lon)
            fill(pad, 0, top, 0, 3, t, lon, up)
            fill(pad, 3, x_ref, 0, 6, t, lon, keep)
            fill(pad, 9, x_ref, 10, 6, t, lon, keep)
            fill(pad, 15, bottom, 0, 3, t, lon, down)
            convbuf[pl.ds(0, 48)] = conv_rows(pad, 0, taps, bias, 3).astype(BF16)
            convbuf[pl.ds(48, 48)] = conv_rows(pad, 9, taps, bias, 3).astype(BF16)

        @pl.when(n > 0)
        def _():
            for cp in copies(before, b):
                cp.start()

        return 0

    @pl.when(count > 0)
    def _():
        lax.fori_loop(0, count + 1, step, 0)
        for d in range(SLOTS, 0, -1):
            @pl.when(count >= d)
            def _():
                for cp in copies(count - d, lax.rem(count - d, SLOTS)):
                    cp.wait()


def block_call(inner, owner, x, halos, consts, sent, levels):
    bands, lon = owner.shape
    vmem = pl.BlockSpec(memory_space=pltpu.VMEM)
    smem = pl.BlockSpec(memory_space=pltpu.SMEM)
    hbm = pl.BlockSpec(memory_space=pltpu.HBM)
    args = [owner, x, *halos, *consts]
    specs = [smem] + [vmem] * (len(args) - 1)
    aliases = {}
    if sent is not None:
        aliases = {len(args): 0}
        args.append(sent)
        specs.append(hbm)
    cells = 160 if inner else 96
    return pl.pallas_call(
        functools.partial(block_kernel, inner),
        in_specs=specs,
        out_specs=hbm,
        out_shape=jax.ShapeDtypeStruct((bands, levels, CAP, TS * TS // levels, C), BF16),
        scratch_shapes=[
            pltpu.VMEM((16 if inner else 18, 32, C), F32),
            pltpu.VMEM((49, 8, C), F32),
            pltpu.VMEM((cells, C), BF16),
            pltpu.VMEM((SLOTS, cells, C), BF16),
            pltpu.SMEM((bands,), jnp.int32),
            pltpu.SMEM((lon + 1,), jnp.int32),
            pltpu.SMEM((lon + 1,), jnp.int32),
            pltpu.SemaphoreType.DMA((SLOTS, 4)),
        ],
        input_output_aliases=aliases,
        compiler_params=pltpu.CompilerParams(vmem_limit_bytes=32 << 20),
        name="inner_rows" if inner else "edge_rows",
    )(*args)


def vertical_kernel(src, rank, recv, w, out, held, done, sem_in, sem_out):
    tiles = held.shape[0]
    levels, cells = held.shape[1], held.shape[2]

    def fetch(t):
        return pltpu.make_async_copy(recv.at[src[t], :, rank[t]], held.at[t], sem_in.at[t])

    def store(t):
        return pltpu.make_async_copy(done.at[t], out.at[t], sem_out.at[t])

    def start(t, _):
        fetch(t).start()
        return 0

    lax.fori_loop(0, tiles, start, 0)

    def step(t, _):
        fetch(t).wait()
        x = held[t].reshape(levels * cells, C)
        zero = jnp.zeros((2 * cells, C), BF16)
        padded = jnp.concatenate([zero, x, zero], axis=0)
        wide = jnp.concatenate(
            [padded[k * cells : (k + levels) * cells] for k in range(5)], axis=1)
        total = x.astype(F32) + jnp.dot(wide, w[...], preferred_element_type=F32)
        done[t] = total.astype(BF16).reshape(levels, cells, C)
        store(t).start()
        return 0

    lax.fori_loop(0, tiles, step, 0)

    def drain(t, _):
        store(t).wait()
        return 0

    lax.fori_loop(0, tiles, drain, 0)


def vertical_call(src, rank, recv, w_vert):
    tiles = src.shape[0]
    levels, cells = recv.shape[1], recv.shape[3]
    smem = pl.BlockSpec(memory_space=pltpu.SMEM)
    hbm = pl.BlockSpec(memory_space=pltpu.HBM)
    return pl.pallas_call(
        vertical_kernel,
        in_specs=[smem, smem, hbm, pl.BlockSpec(memory_space=pltpu.VMEM)],
        out_specs=hbm,
        out_shape=jax.ShapeDtypeStruct((tiles, levels, cells, C), BF16),
        scratch_shapes=[
            pltpu.VMEM((tiles, levels, cells, C), BF16),
            pltpu.VMEM((tiles, levels, cells, C), BF16),
            pltpu.SemaphoreType.DMA((tiles,)),
            pltpu.SemaphoreType.DMA((tiles,)),
        ],
        compiler_params=pltpu.CompilerParams(vmem_limit_bytes=32 << 20),
        name="vertical",
    )(src, rank, recv, w_vert.reshape(5 * C, C))


def body(ocean_state, tile_owner, kernel, bias_dw, ln_gain, ln_bias, w_in, b_in, w_out, b_out,
         layer_scale, w_vert):
    bands, lon = tile_owner.shape
    levels = lax.axis_size("lev")
    band = lax.axis_index("tile")
    x = ocean_state[0]
    ends = bands - 1
    top = lax.ppermute(x[TS - 3 :], "tile", [(i, i + 1) for i in range(ends)])
    bottom = lax.ppermute(x[:3], "tile", [(i + 1, i) for i in range(ends)])
    row = lambda v: v.reshape(1, -1)
    consts = (kernel, row(bias_dw), row(ln_gain), row(ln_bias), w_in, row(b_in), w_out, row(b_out),
              row(layer_scale))
    sent = block_call(True, tile_owner, x, (), consts, None, levels)
    sent = block_call(False, tile_owner, x, (top, bottom), consts, sent, levels)
    cells = TS * TS // levels
    received = lax.all_to_all(
        sent.reshape(bands * levels, CAP * cells, C), ("tile", "lev"), split_axis=0,
        concat_axis=0, tiled=True,
    ).reshape(bands, levels, CAP, cells, C)

    owner_of = jnp.where(tile_owner >= 0, tile_owner // bands, -1)
    mine = owner_of == band
    before = jnp.cumsum(mine.astype(jnp.int32), axis=1) - mine
    hit = (tile_owner.reshape(1, -1) == (band * bands + jnp.arange(bands))[:, None])
    code = jnp.arange(bands, dtype=jnp.int32)[:, None] * CAP + before
    found = jnp.sum(jnp.where(hit, code.reshape(1, -1), 0), axis=1)
    return vertical_call(found // CAP, found % CAP, received, w_vert)


def solution(mesh):
    return jax.shard_map(
        body,
        mesh=mesh,
        in_specs=(P("lev", "tile", None, None),) + (P(),) * 11,
        out_specs=P("tile", None, "lev", None),
        check_vma=False,
    )
```

time: 443 us -> 218 us (0.49)
  other arithmetic: 147 us -> 0.54 us
  matrix products: 117 us -> 0 us
  Pallas kernels: 0 us -> 87.8 us
  blocking collectives: 33.5 us -> 0 us
  local copies, waits for them, and re-layouts: 22.3 us -> 13 us
  waiting for transfers between devices: 105 us -> 96.6 us
  starting transfers between devices: 16.4 us -> 20.9 us
    dot_general x21 -> x0, matrix products: 117 us -> none  [the longest x16 111 us: feed_forward(): branch = jnp.dot(hidden, w_out, preferred_element_type=jnp.float32) + b_out]
    pallas_call x0 -> x3, Pallas kernels: none -> 87.8 us  [the longest x2 77.5 us: block_call(): pl.pallas_call(functools.partial(block_kernel, inner), in_specs=specs, ou...]
    convert_element_type x4 -> x1, other arithmetic: 78.4 us -> 0.02 us  [body(): before = jnp.cumsum(mine.astype(jnp.int32), axis=1) - mine]
    reduce_sum x33 -> x1, other arithmetic: 39.8 us -> 0.21 us  [body(): found = jnp.sum(jnp.where(hit, code.reshape(1, -1), 0), axis=1)]
    all_to_all x1 -> x0, blocking collectives: 33.5 us -> none  [to_columns(): lax.all_to_all(block_mid, 'lev', split_axis=2, concat_axis=1, tiled=True)]
    concatenate x1 -> x0, other arithmetic: 18.6 us -> none  [body(): jnp.concatenate([padded[:, :, -3:], padded, padded[:, :, :3]], axis=2)]
    ppermute x2, waiting for transfers between devices: 11 us -> 0.01 us  [the longest x1 0.01 us: body(): bottom = lax.ppermute(x[:3], 'tile', [(i + 1, i) for i in range(ends)])]
    gather x4 -> x0, local copies, waits for them, and re-layouts: 10.4 us -> none  [the longest x1 5.2 us: body(): selected = band_mid[pick_index]]
  transfers between devices with their start and end apart: 3 -> 3, of which waited for: 3 -> 1; matrix products, arithmetic and copies ran while one was open for 2% -> 0% of each run, Pallas kernels for 0% -> 19%
where the time goes in v1:
time: 218 us; the launch traced here: 219 us
  waiting for transfers between devices  96.6 us (44%)
  Pallas kernels  87.8 us (40%)
  starting transfers between devices  20.9 us (10%)
  local copies, waits for them, and re-layouts  13 us (6%)
    all_to_all x1, waiting for transfers between devices, body(): lax.all_to_all(sent.reshape(bands * levels, CAP * cells, C), ('tile', 'le...  96.6 us
    pallas_call x2, Pallas kernels, block_call(): pl.pallas_call(functools.partial(block_kernel, inner), in_specs=specs, ou...  77.5 us
    all_to_all x1, starting transfers between devices, body(): lax.all_to_all(sent.reshape(bands * levels, CAP * cells, C), ('tile', 'le...  15.2 us
    unnamed x28, local copies, waits for them, and re-layouts  11.3 us
    pallas_call x1, Pallas kernels, vertical_call(): pl.pallas_call(vertical_kernel, in_specs=[smem, smem, hbm, pl.BlockSpec(m...  10.3 us
    ppermute x1, starting transfers between devices, body(): top = lax.ppermute(x[TS - 3:], 'tile', [(i, i + 1) for i in range(ends)])  4.42 us
  transfers between devices with their start and end apart: 3, of which 1 were waited for; matrix products, arithmetic and copies ran while one was open for 0% of the time, Pallas kernels for 19%

profile of v1, /device:TPU:1, one launch (start us, length us, event | category | flops | bytes accessed | tf_op | source)
XLA Modules:
  0.0 219.0 jit_solution(16735176220719343883)
XLA Ops:
  0.0 1.5 slice_bitcast_fusion
  1.5 4.4 %collective-permute-start = (bf16[3,1024,128]{2,1,0:T(8,128)(2,1)S(1)}, bf16[3,1024,128]{2,1,0:T(8,128)(2,1)S(1)}, u32[]{:S(2)}, u32[]{:S(2)}) collective-permute-start(bf16[3,1024,128]{2,1,0:T(8,128)(2,1)S(1)} %get-tuple-element.6), channel_id=1, source_target_pairs={{0,8},{8,16},{16,24},{24,32},{32,40},{40,48},{48,56},{56,64},{64,7... | collective-permute-start | bytes 2359304 | tf_op jit(solution)/shard_map/ppermute | solution.py:281
  5.9 1.3 collective-permute-start.1
  7.2 0.0 copy-start.1
  7.2 2.2 copy-done.1
  9.4 0.0 copy-start.2
  9.4 0.9 copy-done.2
  10.3 0.9 copy-done.3
  11.2 0.7 copy-done.4
  11.9 0.7 copy-done.7
  12.6 0.7 copy-done.8
  13.3 0.7 copy-done.9
  14.0 0.7 copy-done.10
  14.6 0.7 copy-done.11
  15.3 0.7 copy-done.12
  15.9 0.7 copy-done.13
  16.6 42.2 %inner_rows.1.refs_13_ = bf16[32,8,2,32,128]{4,3,2,1,0:T(8,128)(2,1)S(1)} custom-call(s32[32,64]{1,0:T(8,128)S(1)} %copy-done.4, bf16[16,1024,128]{2,1,0:T(8,128)(2,1)S(1)} %bitcast.15, bf16[7,7,128]{2,1,0:T(8,128)(2,1)S(1)} %copy-done.7, f32[1,128]{1,0:T(1,128)S(1)} %bitcast.20, f32[1,128]{1,0:T(1,128)S(1)} %bitcast.22, f32[1,128]{1,0:T(1,128)S(1)} %bitcast.24, ...), custom_call_target="tpu_custom_call" | custom-call | tf_op jit(solution)/shard_map/inner_rows/pallas_call | solution.py:195
  58.8 0.0 collective-permute-done.refs_2_
  58.8 0.0 collective-permute-done.1.refs_3_
  58.9 35.3 %edge_rows.1 = bf16[32,8,2,32,128]{4,3,2,1,0:T(8,128)(2,1)S(1)} custom-call(s32[32,64]{1,0:T(8,128)S(1)} %copy-done.4, bf16[16,1024,128]{2,1,0:T(8,128)(2,1)S(1)} %bitcast.16, bf16[3,1024,128]{2,1,0:T(8,128)(2,1)S(1)} %collective-permute-done.refs_2_, bf16[3,1024,128]{2,1,0:T(8,128)(2,1)S(1)} %collective-permute-done.1.refs_3_, ...), custom_call_target="tpu_custom_call", output_to_operand_aliasing={{}: (13, {})} | custom-call | tf_op jit(solution)/shard_map/edge_rows/pallas_call | solution.py:195
  94.2 0.0 copy-start
  94.2 2.0 copy-done
  96.1 15.2 %all-to-all-start = ((bf16[256,64,128]{2,1,0:T(8,128)(2,1)}), bf16[256,64,128]{2,1,0:T(8,128)(2,1)}, u32[]{:S(2)}, u32[]{:S(2)}) async-start(bf16[256,64,128]{2,1,0:T(8,128)(2,1)} %bitcast.14), calls=%async_computation | async-start | bytes 8388608 | tf_op jit(solution)/shard_map/all_to_all | solution.py:289
  111.4 0.0 copy-done.5
  111.4 0.1 eq.23
  111.5 0.2 reduce_window_sum.11
  111.7 0.1 subtract_add_fusion
  111.8 0.1 broadcast_in_dim.18
  111.9 0.2 select_reduce_fusion
  112.1 96.6 %all-to-all-done = bf16[256,64,128]{2,1,0:T(8,128)(2,1)} async-done(((bf16[256,64,128]{2,1,0:T(8,128)(2,1)}), bf16[256,64,128]{2,1,0:T(8,128)(2,1)}, u32[]{:S(2)}, u32[]{:S(2)}) %all-to-all-start) | async-done | bytes 4194336 | tf_op jit(solution)/shard_map/all_to_all | solution.py:289
  208.7 0.0 copy-done.6
  208.7 10.3 %vertical.1 = bf16[32,8,32,128]{3,2,1,0:T(8,128)(2,1)} custom-call(s32[32]{0:T(128)S(1)} %get-tuple-element.8.src, s32[32]{0:T(128)S(1)} %get-tuple-element.7.rank, bf16[32,8,2,32,128]{4,3,2,1,0:T(8,128)(2,1)} %bitcast.10.recv, bf16[640,128]{1,0:T(8,128)(2,1)S(1)} %bitcast.17), custom_call_target="tpu_custom_call" | custom-call | tf_op jit(solution)/shard_map/vertical/pallas_call | solution.py:258
  (15 shorter events, 0.1 us)
Async XLA Ops:
  1.5 57.4 %collective-permute-start = (bf16[3,1024,128]{2,1,0:T(8,128)(2,1)S(1)}, bf16[3,1024,128]{2,1,0:T(8,128)(2,1)S(1)}, u32[]{:S(2)}, u32[]{:S(2)}) collective-permute-start(bf16[3,1024,128]{2,1,0:T(8,128)(2,1)S(1)} %get-tuple-element.6), channel_id=1, source_target_pairs={{0,8},{8,16},{16,24},{24,32},{32,40},{40,48},{48,56},{56,64},{64,7... | collective-permute-start | bytes 2359304 | tf_op jit(solution)/shard_map/ppermute | solution.py:281
  5.9 52.9 %collective-permute-start.1 = (bf16[3,1024,128]{2,1,0:T(8,128)(2,1)S(1)}, bf16[3,1024,128]{2,1,0:T(8,128)(2,1)S(1)}, u32[]{:S(2)}, u32[]{:S(2)}) collective-permute-start(bf16[3,1024,128]{2,1,0:T(8,128)(2,1)S(1)} %get-tuple-element.5), channel_id=1, source_target_pairs={{8,0},{16,8},{24,16},{32,24},{40,32},{48,40},{56,48},{64,56},{72,6... | collective-permute-start | bytes 2359304 | tf_op jit(solution)/shard_map/ppermute | solution.py:282
  7.2 2.2 %copy-start.1 = (bf16[1,16,1024,128]{3,2,1,0:T(8,128)(2,1)S(1)}, bf16[1,16,1024,128]{3,2,1,0:T(8,128)(2,1)}, u32[]{:S(2)}) copy-start(bf16[1,16,1024,128]{3,2,1,0:T(8,128)(2,1)} %param.12) | copy-start | bytes 12582916
  9.4 0.9 copy-start.2
  10.3 0.9 copy-start.3
  11.2 0.7 copy-start.4
  11.9 0.7 copy-start.7
  12.6 0.7 copy-start.8
  13.3 0.7 copy-start.9
  14.0 0.7 copy-start.10
  14.6 0.7 copy-start.11
  15.3 0.7 copy-start.12
  15.9 0.7 copy-start.13
  94.2 2.0 copy-start
  96.1 15.2 %copy-start.5 = (s32[32,64]{1,0:T(8,128)S(1)}, s32[32,64]{1,0:T(8,128)}, u32[]{:S(2)}) copy-start(s32[32,64]{1,0:T(8,128)} %refs_0_.3) | copy-start | bytes 24580
  96.1 112.6 %copy-start.6 = (bf16[5,128,128]{2,1,0:T(8,128)(2,1)S(1)}, bf16[5,128,128]{2,1,0:T(8,128)(2,1)}, u32[]{:S(2)}) copy-start(bf16[5,128,128]{2,1,0:T(8,128)(2,1)} %param.23) | copy-start | bytes 491524
  96.1 112.6 %all-to-all-start = ((bf16[256,64,128]{2,1,0:T(8,128)(2,1)}), bf16[256,64,128]{2,1,0:T(8,128)(2,1)}, u32[]{:S(2)}, u32[]{:S(2)}) async-start(bf16[256,64,128]{2,1,0:T(8,128)(2,1)} %bitcast.14), calls=%async_computation | async-start | bytes 8388608 | tf_op jit(solution)/shard_map/all_to_all | solution.py:289

commit v2 on v1

v2 whole, which is shorter than its diff:
```python
import functools

import jax
import jax.numpy as jnp
from jax import lax
from jax.experimental import pallas as pl
from jax.experimental.pallas import tpu as pltpu
from jax.sharding import PartitionSpec as P

CAP = 2
TS = 16
C = 128
F32 = jnp.float32
BF16 = jnp.bfloat16
SLOTS = 2
VMEM_BYTES = 63 << 20


def list_wet(owner_ref, band, want, seen, cols, dests):
    bands, lon = owner_ref.shape

    def clear(o, _):
        seen[o] = 0
        return 0

    lax.fori_loop(0, bands, clear, 0)

    def scan(c, count):
        g = owner_ref[band, c]
        dest = lax.shift_right_logical(jnp.maximum(g, 0), bands.bit_length() - 1)
        rank = seen[dest]
        cols[count] = c
        dests[count] = dest
        seen[dest] = rank + (g >= 0).astype(jnp.int32)
        return count + ((g >= 0) & (rank == want)).astype(jnp.int32)

    return lax.fori_loop(0, lon, scan, 0)


def conv_rows(pad_ref, first, taps, bias, rows):
    total = [[bias, bias] for _ in range(rows)]
    for j in range(7):
        ks = [taps[i * 7 + j] for i in range(7)]
        for yi in range(rows + 6):
            for h in range(2):
                v = pad_ref[first + yi, pl.ds(5 + j + 8 * h, 8), :]
                for i in range(7):
                    y = yi - i
                    if 0 <= y < rows:
                        total[y][h] = total[y][h] + v * ks[i]
    return jnp.concatenate([t for pair in total for t in pair], axis=0)


def pointwise(conv, inp, gain, shift, w_in, b_in, w_out, b_out, scale):
    values = conv.astype(F32)
    centre = jnp.mean(values, axis=-1, keepdims=True)
    dev = values - centre
    spread = jnp.mean(dev * dev, axis=-1, keepdims=True)
    normed = (dev * lax.rsqrt(spread + 1e-06) * gain + shift).astype(BF16)
    h = jnp.dot(normed, w_in, preferred_element_type=F32) + b_in
    half = 0.5 * h
    hidden = (half + half * lax.erf(h * 0.7071067811865476)).astype(BF16)
    branch = jnp.dot(hidden, w_out, preferred_element_type=F32) + b_out
    return (inp.astype(F32) + scale * branch).astype(BF16)


def fill(pad_ref, first, src, row0, rows, t, lon, wet):
    left = lax.rem(t + lon - 1, lon)
    right = lax.rem(t + 1, lon)

    def tile(col):
        return src[pl.ds(row0, rows), pl.ds(pl.multiple_of(col * TS, TS), TS), :].astype(F32)

    keep_l, keep_c, keep_r = wet
    zero = jnp.zeros((), F32)
    centre = tile(t)
    if keep_c is not None:
        centre = jnp.where(keep_c, centre, zero)
    pad_ref[pl.ds(first, rows), pl.ds(0, 8), :] = jnp.where(keep_l, tile(left)[:, 8:, :], zero)
    pad_ref[pl.ds(first, rows), pl.ds(8, 16), :] = centre
    pad_ref[pl.ds(first, rows), pl.ds(24, 8), :] = jnp.where(keep_r, tile(right)[:, :8, :], zero)


def neighbours(owner_ref, band, t, lon):
    left = lax.rem(t + lon - 1, lon)
    right = lax.rem(t + 1, lon)
    return (owner_ref[band, left] >= 0, owner_ref[band, t] >= 0, owner_ref[band, right] >= 0)


INNER, EDGES, FULL = "inner_rows", "edge_rows", "full_rows"
CELLS = {INNER: 160, EDGES: 96, FULL: 256}


def block_kernel(rows, want, batch, n_args, n_pass, *refs):
    args, refs = refs[:n_args], refs[n_args + n_pass :]
    send, refs = refs[0], refs[1:]
    held, refs = refs[:n_args], refs[n_args:]
    pad, taps, convbuf, inbuf, stage, seen, cols, dests, sem, load = refs
    loads = []
    for q, (src, dst) in enumerate(zip(args, held)):
        if rows == EDGES and q == 1:
            loads.append(pltpu.make_async_copy(src.at[pl.ds(0, 6)], dst.at[pl.ds(0, 6)], load.at[q]))
            loads.append(pltpu.make_async_copy(src.at[pl.ds(10, 6)], dst.at[pl.ds(6, 6)], load.at[n_args]))
        else:
            loads.append(pltpu.make_async_copy(src, dst, load.at[q]))
    for cp in loads:
        cp.start()
    for cp in loads:
        cp.wait()
    owner_ref, x_ref = held[:2]
    if rows != INNER:
        top, bottom = held[2:4]
    taps_in, bias_ref, gain, shift, w_in, b_in, w_out, b_out, scale = held[-9:]
    bands, lon = owner_ref.shape
    band = lax.axis_index("tile")
    count = list_wet(owner_ref, band, want, seen, cols, dests)
    for i in range(7):
        for j in range(7):
            taps[i * 7 + j] = jnp.broadcast_to(taps_in[i, pl.ds(j, 1), :].astype(F32), (8, C))
    cells = convbuf.shape[1]

    def copies(dest, q, b):
        def piece(p, lo, n, lev, nlev, off, width):
            src = stage.at[b, q, pl.ds(lo, n)]
            if nlev > 1:
                src, dst = src.reshape(nlev, width, C), send.at[dest, pl.ds(lev, nlev)]
            else:
                dst = send.at[dest, lev, pl.ds(off, width)]
            return pltpu.make_async_copy(src, dst, sem.at[b, q, p])

        if rows == FULL:
            return [piece(0, 0, 256, 0, 8, 0, 32)]
        if rows == INNER:
            return [piece(0, 0, 16, 1, 1, 16, 16), piece(1, 16, 128, 2, 4, 0, 32),
                    piece(2, 144, 16, 6, 1, 0, 16)]
        return [piece(0, 0, 32, 0, 1, 0, 32), piece(1, 32, 16, 1, 1, 0, 16),
                piece(2, 48, 16, 6, 1, 16, 16), piece(3, 64, 32, 7, 1, 0, 32)]

    def each_copy(k, b, act):
        for q in range(batch):
            index = k * batch + q

            @pl.when(index < count)
            def _():
                for cp in copies(dests[index], q, b):
                    act(cp)

    def convolve(k, q):
        t = cols[k * batch + q]
        own = neighbours(owner_ref, band, t, lon)
        keep = (own[0], None, own[2])
        bias = jnp.broadcast_to(bias_ref[...], (8, C))
        column = pl.ds(pl.multiple_of(t * TS, TS), TS)
        if rows == INNER:
            inbuf[q] = x_ref[pl.ds(3, 10), column, :].reshape(cells, C)
            fill(pad, 0, x_ref, 0, 16, t, lon, keep)
            convbuf[q] = conv_rows(pad, 0, taps, bias, 10).astype(BF16)
            return
        up = neighbours(owner_ref, jnp.maximum(band - 1, 0), t, lon)
        down = neighbours(owner_ref, jnp.minimum(band + 1, bands - 1), t, lon)
        held_rows = x_ref.shape[0]
        fill(pad, 0, top, 0, 3, t, lon, up)
        fill(pad, 3, x_ref, 0, held_rows, t, lon, keep)
        fill(pad, 3 + held_rows, bottom, 0, 3, t, lon, down)
        if rows == FULL:
            inbuf[q] = x_ref[:, column, :].reshape(cells, C)
            convbuf[q] = conv_rows(pad, 0, taps, bias, 16).astype(BF16)
            return
        inbuf[q, pl.ds(0, 48)] = x_ref[pl.ds(0, 3), column, :].reshape(48, C)
        inbuf[q, pl.ds(48, 48)] = x_ref[pl.ds(9, 3), column, :].reshape(48, C)
        convbuf[q, pl.ds(0, 48)] = conv_rows(pad, 0, taps, bias, 3).astype(BF16)
        convbuf[q, pl.ds(48, 48)] = conv_rows(pad, 9, taps, bias, 3).astype(BF16)

    def step(k, _):
        b = lax.rem(k, SLOTS)

        @pl.when(k >= SLOTS)
        def _():
            each_copy(k - SLOTS, b, lambda cp: cp.wait())

        def one(q, _):
            convolve(k, q)
            return 0

        lax.fori_loop(0, jnp.minimum(batch, count - k * batch), one, 0)
        stage[b] = pointwise(
            convbuf[...].reshape(batch * cells, C), inbuf[...].reshape(batch * cells, C),
            gain[...], shift[...], w_in[...], b_in[...], w_out[...], b_out[...], scale[...],
        ).reshape(batch, cells, C)
        each_copy(k, b, lambda cp: cp.start())
        return 0

    batches = lax.div(count + batch - 1, batch)
    lax.fori_loop(0, batches, step, 0)
    for d in range(SLOTS, 0, -1):
        k = batches - d

        @pl.when(k >= 0)
        def _():
            each_copy(k, lax.rem(k, SLOTS), lambda cp: cp.wait())


def block_call(rows, want, batch, owner, x, halos, consts, levels, alias=None, after=None):
    bands, lon = owner.shape
    hbm = pl.BlockSpec(memory_space=pltpu.HBM)
    args = [owner, x, *halos, *consts]
    n_args = len(args)
    held = [pltpu.SMEM(owner.shape, owner.dtype)]
    held.append(pltpu.VMEM((12 if rows == EDGES else x.shape[0],) + x.shape[1:], x.dtype))
    held += [pltpu.VMEM(v.shape, v.dtype) for v in args[2:]]
    passed = [v for v in (alias, after) if v is not None]
    cells = CELLS[rows]
    return pl.pallas_call(
        functools.partial(block_kernel, rows, want, batch, n_args, len(passed)),
        in_specs=[hbm] * (n_args + len(passed)),
        out_specs=hbm,
        out_shape=jax.ShapeDtypeStruct((bands, levels, TS * TS // levels, C), BF16),
        scratch_shapes=held + [
            pltpu.VMEM((22, 32, C), F32),
            pltpu.VMEM((49, 8, C), F32),
            pltpu.VMEM((batch, cells, C), BF16),
            pltpu.VMEM((batch, cells, C), BF16),
            pltpu.VMEM((SLOTS, batch, cells, C), BF16),
            pltpu.SMEM((bands,), jnp.int32),
            pltpu.SMEM((lon + 1,), jnp.int32),
            pltpu.SMEM((lon + 1,), jnp.int32),
            pltpu.SemaphoreType.DMA((SLOTS, batch, 4)),
            pltpu.SemaphoreType.DMA((n_args + 1,)),
        ],
        input_output_aliases={} if alias is None else {n_args: 0},
        compiler_params=pltpu.CompilerParams(vmem_limit_bytes=VMEM_BYTES),
        cost_estimate=pl.CostEstimate(
            flops=bands * cells * C * (2 * 49 + 4 * 512) * 8, transcendentals=bands * cells * 512,
            bytes_accessed=2 * x.size + bands * cells * C * 2),
        name=rows,
    )(*args, *passed)


GROUP = 4


def vertical_kernel(src, rank, recv0, recv1, w_hbm, out, held, done, w, sem_in, sem_out, sem_w):
    tiles, levels, cells = held.shape[:3]

    def each_fetch(t, act):
        for r, recv in enumerate((recv0, recv1)):
            @pl.when(rank[t] == r)
            def _():
                act(pltpu.make_async_copy(recv.at[src[t]], held.at[t], sem_in.at[t]))

    def store(t):
        return pltpu.make_async_copy(done.at[t], out.at[t], sem_out.at[t])

    def start(t, _):
        each_fetch(t, lambda cp: cp.start())
        return 0

    weights = pltpu.make_async_copy(w_hbm, w, sem_w)
    weights.start()
    lax.fori_loop(0, tiles, start, 0)
    weights.wait()

    def step(g, _):
        for q in range(GROUP):
            each_fetch(g * GROUP + q, lambda cp: cp.wait())
        zero = jnp.zeros((2 * cells, C), BF16)
        centre, wide = [], []
        for q in range(GROUP):
            x = held[g * GROUP + q].reshape(levels * cells, C)
            padded = jnp.concatenate([zero, x, zero], axis=0)
            centre.append(x.astype(F32))
            wide.append(jnp.concatenate(
                [padded[k * cells : (k + levels) * cells] for k in range(5)], axis=1))
        total = jnp.concatenate(centre, axis=0) + jnp.dot(
            jnp.concatenate(wide, axis=0), w[...], preferred_element_type=F32)
        done[pl.ds(g * GROUP, GROUP)] = total.astype(BF16).reshape(GROUP, levels, cells, C)
        for q in range(GROUP):
            store(g * GROUP + q).start()
        return 0

    lax.fori_loop(0, tiles // GROUP, step, 0)

    def drain(t, _):
        store(t).wait()
        return 0

    lax.fori_loop(0, tiles, drain, 0)


def vertical_call(src, rank, recv0, recv1, w_vert):
    tiles = src.shape[0]
    levels, cells = recv0.shape[1:3]
    smem = pl.BlockSpec(memory_space=pltpu.SMEM)
    hbm = pl.BlockSpec(memory_space=pltpu.HBM)
    return pl.pallas_call(
        vertical_kernel,
        in_specs=[smem, smem, hbm, hbm, hbm],
        out_specs=hbm,
        out_shape=jax.ShapeDtypeStruct((tiles, levels, cells, C), BF16),
        scratch_shapes=[
            pltpu.VMEM((tiles, levels, cells, C), BF16),
            pltpu.VMEM((tiles, levels, cells, C), BF16),
            pltpu.VMEM((5 * C, C), BF16),
            pltpu.SemaphoreType.DMA((tiles,)),
            pltpu.SemaphoreType.DMA((tiles,)),
            pltpu.SemaphoreType.DMA,
        ],
        compiler_params=pltpu.CompilerParams(vmem_limit_bytes=VMEM_BYTES),
        name="vertical",
    )(src, rank, recv0, recv1, w_vert.reshape(5 * C, C))


def body(ocean_state, tile_owner, kernel, bias_dw, ln_gain, ln_bias, w_in, b_in, w_out, b_out,
         layer_scale, w_vert):
    bands, lon = tile_owner.shape
    levels = lax.axis_size("lev")
    band = lax.axis_index("tile")
    x = ocean_state[0]
    ends = bands - 1
    top = lax.ppermute(x[TS - 3 :], "tile", [(i, i + 1) for i in range(ends)])
    bottom = lax.ppermute(x[:3], "tile", [(i + 1, i) for i in range(ends)])
    row = lambda v: v.reshape(1, -1)
    consts = (kernel, row(bias_dw), row(ln_gain), row(ln_bias), w_in, row(b_in), w_out, row(b_out),
              row(layer_scale))
    halos = (top, bottom)

    def exchange(sent):
        return lax.all_to_all(
            sent.reshape((bands * levels,) + sent.shape[2:]), ("tile", "lev"), split_axis=0,
            concat_axis=0, tiled=True,
        ).reshape(sent.shape)

    sent1 = block_call(INNER, 1, 4, tile_owner, x, (), consts, levels)
    sent1 = block_call(EDGES, 1, 8, tile_owner, x, halos, consts, levels, alias=sent1)
    sent0 = block_call(FULL, 0, 4, tile_owner, x, halos, consts, levels, after=sent1)
    sent0, recv1 = lax.optimization_barrier((sent0, exchange(sent1)))
    recv0 = exchange(sent0)

    owner_of = jnp.where(tile_owner >= 0, tile_owner // bands, -1)
    mine = owner_of == band
    before = jnp.cumsum(mine.astype(jnp.int32), axis=1) - mine
    hit = (tile_owner.reshape(1, -1) == (band * bands + jnp.arange(bands))[:, None])
    code = jnp.arange(bands, dtype=jnp.int32)[:, None] * CAP + before
    found = jnp.sum(jnp.where(hit, code.reshape(1, -1), 0), axis=1)
    return vertical_call(found // CAP, found % CAP, recv0, recv1, w_vert)


def solution(mesh):
    return jax.shard_map(
        body,
        mesh=mesh,
        in_specs=(P("lev", "tile", None, None),) + (P(),) * 11,
        out_specs=P("tile", None, "lev", None),
        check_vma=False,
    )
```

time: 218 us -> 174 us (0.80)
  Pallas kernels: 87.8 us -> 46.3 us
  starting transfers between devices: 20.9 us -> 36 us
  local copies, waits for them, and re-layouts: 13 us -> 2.51 us
  waiting for transfers between devices: 96.6 us -> 87.9 us
    pallas_call x3 -> x4, Pallas kernels: 87.8 us -> 46.3 us  [the longest x3 39 us: block_call(): pl.pallas_call(functools.partial(block_kernel, rows, want, batch, n_args,...]
    all_to_all x1 -> x2, waiting for transfers between devices: 96.6 us -> 73 us  [exchange(): lax.all_to_all(sent.reshape((bands * levels,) + sent.shape[2:]), ('tile',...]
    all_to_all x1 -> x2, starting transfers between devices: 15.2 us -> 29.4 us  [exchange(): lax.all_to_all(sent.reshape((bands * levels,) + sent.shape[2:]), ('tile',...]
    unnamed x28 -> x2, local copies, waits for them, and re-layouts: 11.3 us -> 0.01 us
    ppermute x1, waiting for transfers between devices: 0.01 us -> 10.5 us  [body(): top = lax.ppermute(x[TS - 3:], 'tile', [(i, i + 1) for i in range(ends)])]
    ppermute x1, waiting for transfers between devices: 0.01 us -> 4.45 us  [body(): bottom = lax.ppermute(x[:3], 'tile', [(i + 1, i) for i in range(ends)])]
  transfers between devices with their start and end apart: 3 -> 4, of which waited for: 1 -> 4; matrix products, arithmetic and copies ran while one was open for 0% -> 1% of each run, Pallas kernels for 19% -> 20%
where the time goes in v2:
time: 174 us
  waiting for transfers between devices  87.9 us (51%)
  Pallas kernels  46.3 us (27%)
  starting transfers between devices  36 us (21%)
  local copies, waits for them, and re-layouts  2.51 us (1%)
    all_to_all x2, waiting for transfers between devices, exchange(): lax.all_to_all(sent.reshape((bands * levels,) + sent.shape[2:]), ('tile',...  73 us
    pallas_call x3, Pallas kernels, block_call(): pl.pallas_call(functools.partial(block_kernel, rows, want, batch, n_args,...  39 us
    all_to_all x2, starting transfers between devices, exchange(): lax.all_to_all(sent.reshape((bands * levels,) + sent.shape[2:]), ('tile',...  29.4 us
    ppermute x1, waiting for transfers between devices, body(): top = lax.ppermute(x[TS - 3:], 'tile', [(i, i + 1) for i in range(ends)])  10.5 us
    pallas_call x1, Pallas kernels, vertical_call(): pl.pallas_call(vertical_kernel, in_specs=[smem, smem, hbm, hbm, hbm], out...  7.28 us
    ppermute x1, starting transfers between devices, body(): top = lax.ppermute(x[TS - 3:], 'tile', [(i, i + 1) for i in range(ends)])  5.25 us
    ppermute x1, waiting for transfers between devices, body(): bottom = lax.ppermute(x[:3], 'tile', [(i + 1, i) for i in range(ends)])  4.45 us
  transfers between devices with their start and end apart: 4, of which 4 were waited for; matrix products, arithmetic and copies ran while one was open for 1% of the time, Pallas kernels for 20%

profile of v2, /device:TPU:1, one launch (start us, length us, event | category | flops | bytes accessed | tf_op | source)
XLA Modules:
  0.0 173.9 jit_solution(8438762620906520320)
XLA Ops:
  0.0 2.4 %slice_bitcast_fusion = (bf16[3,1024,128]{2,1,0:T(8,128)(2,1)S(1)}, bf16[3,1024,128]{2,1,0:T(8,128)(2,1)}) fusion(bf16[1,16,1024,128]{3,2,1,0:T(8,128)(2,1)} %param.12), kind=kLoop, calls=%fused_computation | loop fusion | bytes 3145728 | tf_op jit(solution)/shard_map/slice | solution.py:321
  2.4 5.2 %collective-permute-start = (bf16[3,1024,128]{2,1,0:T(8,128)(2,1)}, bf16[3,1024,128]{2,1,0:T(8,128)(2,1)}, u32[]{:S(2)}, u32[]{:S(2)}) collective-permute-start(bf16[3,1024,128]{2,1,0:T(8,128)(2,1)} %get-tuple-element.10), channel_id=1, source_target_pairs={{0,8},{8,16},{16,24},{24,32},{32,40},{40,48},{48,56},{56,64},{64,7... | collective-permute-start | bytes 2359304 | tf_op jit(solution)/shard_map/ppermute | solution.py:320
  7.6 1.3 collective-permute-start.1
  8.9 3.9 %inner_rows.1.refs_13_ = bf16[32,8,32,128]{3,2,1,0:T(8,128)(2,1)} custom-call(s32[32,64]{1,0:T(8,128)} %refs_0_.5, bf16[16,1024,128]{2,1,0:T(8,128)(2,1)} %bitcast.18, bf16[7,7,128]{2,1,0:T(8,128)(2,1)} %refs_4_.3, f32[1,128]{1,0:T(1,128)} %bitcast.25, f32[1,128]{1,0:T(1,128)} %bitcast.28, f32[1,128]{1,0:T(1,128)} %bitcast.31, bf16[128,512]{1,0:T(8,128)(2,1)} %refs_8_.5, ...), custom_call_target="tpu_custom_call" | custom-call | flops 11251220480 | bytes 5505024 | tf_op jit(solution)/shard_map/inner_rows/pallas_call | solution.py:213
  12.8 10.5 %collective-permute-done.refs_2_ = bf16[3,1024,128]{2,1,0:T(8,128)(2,1)} collective-permute-done((bf16[3,1024,128]{2,1,0:T(8,128)(2,1)}, bf16[3,1024,128]{2,1,0:T(8,128)(2,1)}, u32[]{:S(2)}, u32[]{:S(2)}) %collective-permute-start) | collective-permute-done | bytes 786464 | tf_op jit(solution)/shard_map/ppermute | solution.py:320
  23.2 4.5 %collective-permute-done.1.refs_3_ = bf16[3,1024,128]{2,1,0:T(8,128)(2,1)} collective-permute-done((bf16[3,1024,128]{2,1,0:T(8,128)(2,1)S(1)}, bf16[3,1024,128]{2,1,0:T(8,128)(2,1)}, u32[]{:S(2)}, u32[]{:S(2)}) %collective-permute-start.1) | collective-permute-done | bytes 786464 | tf_op jit(solution)/shard_map/ppermute | solution.py:321
  27.7 4.3 %edge_rows.1.refs_13_ = bf16[32,8,32,128]{3,2,1,0:T(8,128)(2,1)} custom-call(s32[32,64]{1,0:T(8,128)} %refs_0_.5, bf16[16,1024,128]{2,1,0:T(8,128)(2,1)} %bitcast.19, bf16[3,1024,128]{2,1,0:T(8,128)(2,1)} %collective-permute-done.refs_2_, bf16[3,1024,128]{2,1,0:T(8,128)(2,1)} %collective-permute-done.1.refs_3_, ...), custom_call_target="tpu_custom_call", output_to_operand_aliasing={{}: (13, {})} | custom-call | flops 6750732288 | bytes 4980736 | tf_op jit(solution)/shard_map/edge_rows/pallas_call | solution.py:213
  32.0 21.9 %all-to-all-start = ((bf16[256,32,128]{2,1,0:T(8,128)(2,1)}), bf16[256,32,128]{2,1,0:T(8,128)(2,1)}, u32[]{:S(2)}, u32[]{:S(2)}) async-start(bf16[256,32,128]{2,1,0:T(8,128)(2,1)} %bitcast.17), calls=%async_computation | async-start | bytes 4194304 | tf_op jit(solution)/shard_map/all_to_all | solution.py:328
  54.0 30.8 %full_rows.1 = bf16[32,8,32,128]{3,2,1,0:T(8,128)(2,1)} custom-call(s32[32,64]{1,0:T(8,128)} %refs_0_.5, bf16[16,1024,128]{2,1,0:T(8,128)(2,1)} %bitcast.20, bf16[3,1024,128]{2,1,0:T(8,128)(2,1)} %collective-permute-done.refs_2_, bf16[3,1024,128]{2,1,0:T(8,128)(2,1)} %collective-permute-done.1.refs_3_, bf16[7,7,128]{2,1,0:T(8,128)(2,1)} %refs_4_.3, ...), custom_call_target="tpu_custom_call" | custom-call | flops 18001952768 | bytes 6291456 | tf_op jit(solution)/shard_map/full_rows/pallas_call | solution.py:213
  84.8 21.7 %all-to-all-done = bf16[256,32,128]{2,1,0:T(8,128)(2,1)} async-done(((bf16[256,32,128]{2,1,0:T(8,128)(2,1)}), bf16[256,32,128]{2,1,0:T(8,128)(2,1)}, u32[]{:S(2)}, u32[]{:S(2)}) %all-to-all-start) | async-done | bytes 2097184 | tf_op jit(solution)/shard_map/all_to_all | solution.py:328
  106.5 0.0 copy-start
  106.5 7.5 %all-to-all-start.1 = ((bf16[256,32,128]{2,1,0:T(8,128)(2,1)}), bf16[256,32,128]{2,1,0:T(8,128)(2,1)}, u32[]{:S(2)}, u32[]{:S(2)}) async-start(bf16[256,32,128]{2,1,0:T(8,128)(2,1)} %bitcast.16), calls=%async_computation.1 | async-start | bytes 4194304 | tf_op jit(solution)/shard_map/all_to_all | solution.py:328
  114.0 0.0 copy-done
  114.0 0.1 eq.23
  114.1 0.2 reduce_window_sum.11
  114.3 0.1 subtract_add_fusion
  114.4 0.1 broadcast_in_dim.18
  114.5 0.2 select_reduce_fusion
  114.7 0.6 and_select_fusion
  115.3 51.3 %all-to-all-done.1 = bf16[256,32,128]{2,1,0:T(8,128)(2,1)} async-done(((bf16[256,32,128]{2,1,0:T(8,128)(2,1)}), bf16[256,32,128]{2,1,0:T(8,128)(2,1)}, u32[]{:S(2)}, u32[]{:S(2)}) %all-to-all-start.1) | async-done | bytes 2097184 | tf_op jit(solution)/shard_map/all_to_all | solution.py:328
  166.6 7.3 %vertical.1 = bf16[32,8,32,128]{3,2,1,0:T(8,128)(2,1)} custom-call(s32[32]{0:T(128)} %get-tuple-element.12.src, s32[32]{0:T(128)} %get-tuple-element.11.rank, bf16[32,8,32,128]{3,2,1,0:T(8,128)(2,1)} %bitcast.12.recv0, bf16[32,8,32,128]{3,2,1,0:T(8,128)(2,1)} %bitcast.10.recv1, bf16[640,128]{1,0:T(8,128)(2,1)} %bitcast.21), custom_call_target="tpu_custom_call" | custom-call | tf_op jit(solution)/shard_map/vertical/pallas_call | solution.py:295
  (3 shorter events, 0.0 us)
Async XLA Ops:
  2.4 20.9 %collective-permute-start = (bf16[3,1024,128]{2,1,0:T(8,128)(2,1)}, bf16[3,1024,128]{2,1,0:T(8,128)(2,1)}, u32[]{:S(2)}, u32[]{:S(2)}) collective-permute-start(bf16[3,1024,128]{2,1,0:T(8,128)(2,1)} %get-tuple-element.10), channel_id=1, source_target_pairs={{0,8},{8,16},{16,24},{24,32},{32,40},{40,48},{48,56},{56,64},{64,7... | collective-permute-start | bytes 2359304 | tf_op jit(solution)/shard_map/ppermute | solution.py:320
  7.6 20.1 %collective-permute-start.1 = (bf16[3,1024,128]{2,1,0:T(8,128)(2,1)S(1)}, bf16[3,1024,128]{2,1,0:T(8,128)(2,1)}, u32[]{:S(2)}, u32[]{:S(2)}) collective-permute-start(bf16[3,1024,128]{2,1,0:T(8,128)(2,1)S(1)} %get-tuple-element.9), channel_id=1, source_target_pairs={{8,0},{16,8},{24,16},{32,24},{40,32},{48,40},{56,48},{64,56},{72,6... | collective-permute-start | bytes 2359304 | tf_op jit(solution)/shard_map/ppermute | solution.py:321
  32.0 74.4 %all-to-all-start = ((bf16[256,32,128]{2,1,0:T(8,128)(2,1)}), bf16[256,32,128]{2,1,0:T(8,128)(2,1)}, u32[]{:S(2)}, u32[]{:S(2)}) async-start(bf16[256,32,128]{2,1,0:T(8,128)(2,1)} %bitcast.17), calls=%async_computation | async-start | bytes 4194304 | tf_op jit(solution)/shard_map/all_to_all | solution.py:328
  106.5 7.6 %copy-start = (s32[32,64]{1,0:T(8,128)S(1)}, s32[32,64]{1,0:T(8,128)}, u32[]{:S(2)}) copy-start(s32[32,64]{1,0:T(8,128)} %refs_0_.5) | copy-start | bytes 24580
  106.5 60.2 %all-to-all-start.1 = ((bf16[256,32,128]{2,1,0:T(8,128)(2,1)}), bf16[256,32,128]{2,1,0:T(8,128)(2,1)}, u32[]{:S(2)}, u32[]{:S(2)}) async-start(bf16[256,32,128]{2,1,0:T(8,128)(2,1)} %bitcast.16), calls=%async_computation.1 | async-start | bytes 4194304 | tf_op jit(solution)/shard_map/all_to_all | solution.py:328

commit v3 on v2

v3 whole, which is shorter than its diff:
```python
import functools
from fractions import Fraction

import jax
import jax.numpy as jnp
from jax import lax
from jax.experimental import pallas as pl
from jax.experimental.pallas import tpu as pltpu
from jax.sharding import PartitionSpec as P

CAP = 2
TS = 16
C = 128
F32 = jnp.float32
BF16 = jnp.bfloat16
SLOTS = 2
VMEM_BYTES = 63 << 20


def list_wet(owner_ref, band, want, seen, cols, dests):
    bands, lon = owner_ref.shape

    def clear(o, _):
        seen[o] = 0
        return 0

    lax.fori_loop(0, bands, clear, 0)

    def scan(c, count):
        g = owner_ref[band, c]
        dest = lax.shift_right_logical(jnp.maximum(g, 0), bands.bit_length() - 1)
        rank = seen[dest]
        cols[count] = c
        dests[count] = dest
        seen[dest] = rank + (g >= 0).astype(jnp.int32)
        return count + ((g >= 0) & (rank == want)).astype(jnp.int32)

    return lax.fori_loop(0, lon, scan, 0, unroll=4)


def toom_cook():
    pairs = [Fraction(1), Fraction(2), Fraction(1, 2), Fraction(3, 4)]
    squares = [p * p for p in pairs]

    def times(poly, root):
        low = [-root * v for v in poly] + [Fraction(0)]
        high = [Fraction(0)] + list(poly)
        return [p + q for p, q in zip(low, high)]

    def product(roots):
        poly = [Fraction(1)]
        for root in roots:
            poly = times(poly, root)
        return poly

    points = [Fraction(0)] + [v for p in pairs for v in (p, -p)]
    taps = []
    for p in points:
        scale = Fraction(1)
        for q in points:
            if q != p:
                scale = scale * (p - q)
        taps.append([float(p**i / scale) for i in range(7)])
    taps.append([0.0] * 6 + [1.0])
    inner = [[float(v) for v in product([q for q in squares if q != p])] for p in squares]
    whole = [float(v) for v in product(squares)]
    return [float(p) for p in pairs], taps, inner, whole


PAIRS, TAPS, INNER_POLY, WHOLE_POLY = toom_cook()
POINTS = len(TAPS)


def combine(values, coefs):
    total = None
    for v, c in zip(values, coefs):
        term = v if c == 1.0 else v * c
        total = term if total is None else total + term
    return total


def conv_blocks(blocks, wide, taps, bias):
    for m, d in enumerate(blocks):
        values = [combine(d[0:9:2], WHOLE_POLY)]
        for p, poly in zip(PAIRS, INNER_POLY):
            even = combine(d[2:9:2], poly)
            odd = combine(d[1:8:2], poly)
            if p != 1.0:
                odd = odd * p
            values += [even + odd, even - odd]
        values.append(combine(d[1:10:2], WHOLE_POLY))
        for n, v in enumerate(values):
            wide[m, n, pl.ds(0, 8), :] = v[16:]
            wide[m, n, pl.ds(8, 16), :] = v[:16]
            wide[m, n, pl.ds(24, 8), :] = v[16:]
    cells = [(m, h) for m in range(len(blocks)) for h in range(2)]

    def product(n):
        total = [None] * len(cells)
        for j in range(7):
            tap = taps[n * 7 + j]
            for i, (m, h) in enumerate(cells):
                term = wide[m, n, pl.ds(5 + j + 8 * h, 8), :] * tap
                total[i] = term if j == 0 else total[i] + term
        return total

    y = [[v + bias for v in product(0)]] + [[bias] * len(cells) for _ in range(3)]
    for q, p in enumerate(PAIRS):
        plus, minus = product(1 + 2 * q), product(2 + 2 * q)
        for i in range(len(cells)):
            s, t = plus[i] + minus[i], plus[i] - minus[i]
            y[0][i] = y[0][i] + s
            y[1][i] = y[1][i] + (t if p == 1.0 else t * p)
            y[2][i] = y[2][i] + (s if p == 1.0 else s * (p * p))
            y[3][i] = y[3][i] + (t if p == 1.0 else t * (p * p * p))
    last = product(POINTS - 1)
    y[3] = [v + w for v, w in zip(y[3], last)]
    return [[jnp.concatenate([y[r][2 * m], y[r][2 * m + 1]], axis=0) for r in range(4)]
            for m in range(len(blocks))]


def pointwise(conv, inp, gain, shift, w_in, b_in, w_out, b_out, scale):
    values = conv.astype(F32)
    centre = jnp.mean(values, axis=-1, keepdims=True)
    dev = values - centre
    spread = jnp.mean(dev * dev, axis=-1, keepdims=True)
    normed = (dev * lax.rsqrt(spread + 1e-06) * gain + shift).astype(BF16)
    h = jnp.dot(normed, w_in, preferred_element_type=F32) + b_in
    half = 0.5 * h
    hidden = (half + half * lax.erf(h * 0.7071067811865476)).astype(BF16)
    branch = jnp.dot(hidden, w_out, preferred_element_type=F32) + b_out
    return (inp.astype(F32) + scale * branch).astype(BF16)


def window_rows(src, rows, t, lon, keep):
    left = lax.rem(t + lon - 1, lon)
    right = lax.rem(t + 1, lon)
    keep_l, keep_c, keep_r = keep
    zero = jnp.zeros((), F32)
    first = lax.broadcasted_iota(jnp.int32, (8, C), 0) < 4
    keep_side = jnp.where(first, keep_r.astype(F32), keep_l.astype(F32)) > 0

    def tile(r, col):
        return src[r, pl.ds(pl.multiple_of(col * TS, TS), TS), :].astype(F32)

    out = []
    for r in rows:
        centre = tile(r, t)
        if keep_c is not None:
            centre = jnp.where(keep_c, centre, zero)
        side = jnp.where(first, tile(r, right)[:8], tile(r, left)[8:])
        out.append(jnp.concatenate([centre, jnp.where(keep_side, side, zero)], axis=0))
    return out


def neighbours(owner_ref, band, t, lon):
    left = lax.rem(t + lon - 1, lon)
    right = lax.rem(t + 1, lon)
    return (owner_ref[band, left] >= 0, owner_ref[band, t] >= 0, owner_ref[band, right] >= 0)


INNER, EDGES, FULL = "inner_rows", "edge_rows", "full_rows"
CELLS = {INNER: 128, EDGES: 128, FULL: 256}


def block_kernel(rows, want, batch, n_args, n_pass, *refs):
    args, refs = refs[:n_args], refs[n_args + n_pass :]
    send, refs = refs[0], refs[1:]
    held, refs = refs[:n_args], refs[n_args:]
    wide, taps, convbuf, inbuf, stage, seen, cols, dests, sem, load = refs
    loads = []
    for q, (src, dst) in enumerate(zip(args, held)):
        if rows == EDGES and q == 1:
            loads.append(pltpu.make_async_copy(src.at[pl.ds(0, 7)], dst.at[pl.ds(0, 7)], load.at[q]))
            loads.append(pltpu.make_async_copy(src.at[pl.ds(9, 7)], dst.at[pl.ds(7, 7)], load.at[n_args]))
        else:
            loads.append(pltpu.make_async_copy(src, dst, load.at[q]))
    for cp in loads:
        cp.start()
    owner_ref, x_ref = held[:2]
    if rows != INNER:
        top, bottom = held[2:4]
    taps_in, bias_ref, gain, shift, w_in, b_in, w_out, b_out, scale = held[-9:]
    bands, lon = owner_ref.shape
    band = lax.axis_index("tile")
    loads[0].wait()
    count = list_wet(owner_ref, band, want, seen, cols, dests)
    loads[-9].wait()
    for j in range(7):
        column_taps = [
            jnp.broadcast_to(taps_in[i, pl.ds(j, 1), :].astype(F32), (8, C)) for i in range(7)]
        for n in range(POINTS):
            used = [(k, c) for k, c in zip(column_taps, TAPS[n]) if c != 0.0]
            total = combine(*zip(*used))
            taps[n * 7 + j] = total
    for cp in loads[1:-9] + loads[-8:]:
        cp.wait()
    cells = convbuf.shape[1]

    def copies(dest, q, b):
        def piece(p, lo, n, lev):
            return pltpu.make_async_copy(
                stage.at[b, q, pl.ds(lo, n)], send.at[dest, pl.ds(lev, n)], sem.at[b, q, p])

        half = send.shape[1] // 2
        if rows == FULL:
            return [piece(0, 0, 2 * half, 0)]
        if rows == INNER:
            return [piece(0, 0, half, half // 2)]
        return [piece(0, 0, half // 2, 0), piece(1, half // 2, half // 2, half + half // 2)]

    def each_copy(k, b, act):
        for q in range(batch):
            index = k * batch + q

            @pl.when(index < count)
            def _():
                for cp in copies(dests[index], q, b):
                    act(cp)

    def convolve(k, q):
        t = cols[k * batch + q]
        own = neighbours(owner_ref, band, t, lon)
        own = (own[0], None, own[2])
        bias = jnp.broadcast_to(bias_ref[...], (8, C))
        column = pl.ds(pl.multiple_of(t * TS, TS), TS)

        def window(src, picked, keep=own):
            return window_rows(src, picked, t, lon, keep)

        def above(n):
            up = neighbours(owner_ref, jnp.maximum(band - 1, 0), t, lon)
            return window(top, range(3), up) + window(x_ref, range(n))

        def below(n):
            down = neighbours(owner_ref, jnp.minimum(band + 1, bands - 1), t, lon)
            last = x_ref.shape[0]
            return window(x_ref, range(last - n, last)) + window(bottom, range(3), down)

        def put(first, blocks):
            for n, block in enumerate(conv_blocks(blocks, wide, taps, bias)):
                for r, out in enumerate(block):
                    convbuf[q, pl.ds((first + n * 4 + r) * TS, TS)] = out.astype(BF16)

        if rows == INNER:
            cut = window(x_ref, range(1, 15))
            put(0, [cut[:10], cut[4:]])
            inbuf[q] = x_ref[pl.ds(4, 8), column, :].reshape(cells, C)
        elif rows == EDGES:
            put(0, [above(7), below(7)])
            inbuf[q, pl.ds(0, 64)] = x_ref[pl.ds(0, 4), column, :].reshape(64, C)
            inbuf[q, pl.ds(64, 64)] = x_ref[pl.ds(10, 4), column, :].reshape(64, C)
        else:
            cut = above(11)
            put(0, [cut[:10], cut[4:]])
            cut = below(11)
            put(8, [cut[:10], cut[4:]])
            inbuf[q] = x_ref[:, column, :].reshape(cells, C)

    def step(k, _):
        b = lax.rem(k, SLOTS)

        @pl.when(k >= SLOTS)
        def _():
            each_copy(k - SLOTS, b, lambda cp: cp.wait())

        def one(q, _):
            convolve(k, q)
            return 0

        lax.fori_loop(0, jnp.minimum(batch, count - k * batch), one, 0)
        tiles = 512 // cells
        for part in range(0, batch, tiles):
            piece = pl.ds(part, tiles)
            stage[b, piece] = pointwise(
                convbuf[piece].reshape(512, C), inbuf[piece].reshape(512, C), gain[...], shift[...],
                w_in[...], b_in[...], w_out[...], b_out[...], scale[...],
            ).reshape((tiles,) + stage.shape[2:])
        each_copy(k, b, lambda cp: cp.start())
        return 0

    batches = lax.div(count + batch - 1, batch)
    lax.fori_loop(0, batches, step, 0)
    for d in range(SLOTS, 0, -1):
        k = batches - d

        @pl.when(k >= 0)
        def _():
            each_copy(k, lax.rem(k, SLOTS), lambda cp: cp.wait())


def block_call(rows, want, batch, owner, x, halos, consts, levels, alias=None, after=None):
    bands, lon = owner.shape
    hbm = pl.BlockSpec(memory_space=pltpu.HBM)
    args = [owner, x, *halos, *consts]
    n_args = len(args)
    held = [pltpu.SMEM(owner.shape, owner.dtype)]
    held.append(pltpu.VMEM((14 if rows == EDGES else x.shape[0],) + x.shape[1:], x.dtype))
    held += [pltpu.VMEM(v.shape, v.dtype) for v in args[2:]]
    passed = [v for v in (alias, after) if v is not None]
    cells = CELLS[rows]
    share = TS * TS // levels
    return pl.pallas_call(
        functools.partial(block_kernel, rows, want, batch, n_args, len(passed)),
        in_specs=[hbm] * (n_args + len(passed)),
        out_specs=hbm,
        out_shape=jax.ShapeDtypeStruct((bands, levels, share, C), BF16),
        scratch_shapes=held + [
            pltpu.VMEM((2, POINTS, 32, C), F32),
            pltpu.VMEM((POINTS * 7, 8, C), F32),
            pltpu.VMEM((batch, cells, C), BF16),
            pltpu.VMEM((batch, cells, C), BF16),
            pltpu.VMEM((SLOTS, batch, cells // share, share, C), BF16),
            pltpu.SMEM((bands,), jnp.int32),
            pltpu.SMEM((lon + 1,), jnp.int32),
            pltpu.SMEM((lon + 1,), jnp.int32),
            pltpu.SemaphoreType.DMA((SLOTS, batch, 2)),
            pltpu.SemaphoreType.DMA((n_args + 1,)),
        ],
        input_output_aliases={} if alias is None else {n_args: 0},
        compiler_params=pltpu.CompilerParams(vmem_limit_bytes=VMEM_BYTES),
        cost_estimate=pl.CostEstimate(
            flops=bands * cells * C * (2 * 49 + 4 * 512) * 8, transcendentals=bands * cells * 512,
            bytes_accessed=2 * x.size + bands * cells * C * 2),
        name=rows,
    )(*args, *passed)


GROUP = 4


def vertical_kernel(src, rank, recv0, recv1, w_hbm, out, held, done, taps, w, sem_in,
                    sem_out, sem_w):
    tiles, levels, cells = held.shape[:3]

    def each_fetch(t, act):
        for r, recv in enumerate((recv0, recv1)):
            @pl.when(rank[t] == r)
            def _():
                act(pltpu.make_async_copy(recv.at[src[t]], held.at[t], sem_in.at[t]))

    def store(t):
        return pltpu.make_async_copy(done.at[t], out.at[t], sem_out.at[t])

    def start(t, _):
        each_fetch(t, lambda cp: cp.start())
        return 0

    weights = pltpu.make_async_copy(w_hbm, taps, sem_w)
    weights.start()
    lax.fori_loop(0, tiles, start, 0)
    weights.wait()
    for d in range(6):
        for p in range(2):
            k = d - p
            block = taps[k] if 0 <= k < 5 else jnp.zeros((C, C), BF16)
            w[pl.ds(d * C, C), pl.ds(p * C, C)] = block

    def step(g, _):
        for q in range(GROUP):
            each_fetch(g * GROUP + q, lambda cp: cp.wait())
        zero = jnp.zeros((cells, C), BF16)
        wide = []
        for q in range(GROUP):
            x = [zero, zero] + [held[g * GROUP + q, lev] for lev in range(levels)] + [zero, zero]
            wide += [jnp.concatenate(x[lev : lev + 6], axis=1) for lev in range(0, levels, 2)]
        total = jnp.dot(jnp.concatenate(wide, axis=0), w[...], preferred_element_type=F32)
        for q in range(GROUP):
            t = g * GROUP + q
            for lev in range(levels):
                row = (q * levels // 2 + lev // 2) * cells
                part = total[row : row + cells, (lev % 2) * C : (lev % 2 + 1) * C]
                done[t, lev] = (held[t, lev].astype(F32) + part).astype(BF16)
            store(t).start()
        return 0

    lax.fori_loop(0, tiles // GROUP, step, 0)

    def drain(t, _):
        store(t).wait()
        return 0

    lax.fori_loop(0, tiles, drain, 0)


def vertical_call(src, rank, recv0, recv1, w_vert):
    tiles = src.shape[0]
    levels, cells = recv0.shape[1:3]
    smem = pl.BlockSpec(memory_space=pltpu.SMEM)
    hbm = pl.BlockSpec(memory_space=pltpu.HBM)
    return pl.pallas_call(
        vertical_kernel,
        in_specs=[smem, smem, hbm, hbm, hbm],
        out_specs=hbm,
        out_shape=jax.ShapeDtypeStruct((tiles, levels, cells, C), BF16),
        scratch_shapes=[
            pltpu.VMEM((tiles, levels, cells, C), BF16),
            pltpu.VMEM((tiles, levels, cells, C), BF16),
            pltpu.VMEM((5, C, C), BF16),
            pltpu.VMEM((6 * C, 2 * C), BF16),
            pltpu.SemaphoreType.DMA((tiles,)),
            pltpu.SemaphoreType.DMA((tiles,)),
            pltpu.SemaphoreType.DMA,
        ],
        compiler_params=pltpu.CompilerParams(vmem_limit_bytes=VMEM_BYTES),
        name="vertical",
    )(src, rank, recv0, recv1, w_vert)


def body(ocean_state, tile_owner, kernel, bias_dw, ln_gain, ln_bias, w_in, b_in, w_out, b_out,
         layer_scale, w_vert):
    bands, lon = tile_owner.shape
    levels = lax.axis_size("lev")
    band = lax.axis_index("tile")
    x = ocean_state[0]
    ends = bands - 1
    top = lax.ppermute(x[TS - 3 :], "tile", [(i, i + 1) for i in range(ends)])
    bottom = lax.ppermute(x[:3], "tile", [(i + 1, i) for i in range(ends)])
    row = lambda v: v.reshape(1, -1)
    consts = (kernel, row(bias_dw), row(ln_gain), row(ln_bias), w_in, row(b_in), w_out, row(b_out),
              row(layer_scale))
    halos = (top, bottom)

    def exchange(sent):
        return lax.all_to_all(
            sent.reshape((bands * levels,) + sent.shape[2:]), ("tile", "lev"), split_axis=0,
            concat_axis=0, tiled=True,
        ).reshape(sent.shape)

    sent1 = block_call(INNER, 1, 4, tile_owner, x, (), consts, levels)
    sent1 = block_call(EDGES, 1, 4, tile_owner, x, halos, consts, levels, alias=sent1)
    sent0 = block_call(FULL, 0, 4, tile_owner, x, halos, consts, levels, after=sent1)
    sent0, recv1 = lax.optimization_barrier((sent0, exchange(sent1)))
    recv0 = exchange(sent0)

    owner_of = jnp.where(tile_owner >= 0, tile_owner // bands, -1)
    mine = owner_of == band
    before = jnp.cumsum(mine.astype(jnp.int32), axis=1) - mine
    hit = (tile_owner.reshape(1, -1) == (band * bands + jnp.arange(bands))[:, None])
    code = jnp.arange(bands, dtype=jnp.int32)[:, None] * CAP + before
    found = jnp.sum(jnp.where(hit, code.reshape(1, -1), 0), axis=1)
    return vertical_call(found // CAP, found % CAP, recv0, recv1, w_vert)


def solution(mesh):
    return jax.shard_map(
        body,
        mesh=mesh,
        in_specs=(P("lev", "tile", None, None),) + (P(),) * 11,
        out_specs=P("tile", None, "lev", None),
        check_vma=False,
    )
```

time: 174 us -> 170 us (0.977)
  Pallas kernels: 46.3 us -> 37 us
  waiting for transfers between devices: 87.9 us -> 94.6 us
    pallas_call x3, Pallas kernels: 39 us -> 30.9 us  [block_call(): pl.pallas_call(functools.partial(block_kernel, rows, want, batch, n_args,...]
    all_to_all x2, waiting for transfers between devices: 73 us -> 78.3 us  [exchange(): lax.all_to_all(sent.reshape((bands * levels,) + sent.shape[2:]), ('tile',...]
  transfers between devices with their start and end apart: 4 -> 4, of which waited for: 4 -> 4; matrix products, arithmetic and copies ran while one was open for 1% -> 1% of each run, Pallas kernels for 20% -> 16%
where the time goes in v3:
time: 170 us; the launch traced here: 171 us
  waiting for transfers between devices  94.6 us (56%)
  Pallas kernels  37 us (22%)
  starting transfers between devices  35.4 us (21%)
  local copies, waits for them, and re-layouts  2.51 us (1%)
    all_to_all x2, waiting for transfers between devices, exchange(): lax.all_to_all(sent.reshape((bands * levels,) + sent.shape[2:]), ('tile',...  78.3 us
    pallas_call x3, Pallas kernels, block_call(): pl.pallas_call(functools.partial(block_kernel, rows, want, batch, n_args,...  30.9 us
    all_to_all x2, starting transfers between devices, exchange(): lax.all_to_all(sent.reshape((bands * levels,) + sent.shape[2:]), ('tile',...  28.8 us
    ppermute x1, waiting for transfers between devices, body(): top = lax.ppermute(x[TS - 3:], 'tile', [(i, i + 1) for i in range(ends)])  11.8 us
    pallas_call x1, Pallas kernels, vertical_call(): pl.pallas_call(vertical_kernel, in_specs=[smem, smem, hbm, hbm, hbm], out...  6.12 us
    ppermute x1, starting transfers between devices, body(): top = lax.ppermute(x[TS - 3:], 'tile', [(i, i + 1) for i in range(ends)])  5.25 us
    ppermute x1, waiting for transfers between devices, body(): bottom = lax.ppermute(x[:3], 'tile', [(i + 1, i) for i in range(ends)])  4.45 us
  transfers between devices with their start and end apart: 4, of which 4 were waited for; matrix products, arithmetic and copies ran while one was open for 1% of the time, Pallas kernels for 16%

profile of v3, /device:TPU:1, one launch (start us, length us, event | category | flops | bytes accessed | tf_op | source)
XLA Modules:
  0.0 170.7 jit_solution(4138777135061745059)
XLA Ops:
  0.0 2.4 %slice_bitcast_fusion = (bf16[3,1024,128]{2,1,0:T(8,128)(2,1)S(1)}, bf16[3,1024,128]{2,1,0:T(8,128)(2,1)}) fusion(bf16[1,16,1024,128]{3,2,1,0:T(8,128)(2,1)} %param.12), kind=kLoop, calls=%fused_computation | loop fusion | bytes 3145728 | tf_op jit(solution)/shard_map/slice | solution.py:418
  2.4 5.2 %collective-permute-start = (bf16[3,1024,128]{2,1,0:T(8,128)(2,1)}, bf16[3,1024,128]{2,1,0:T(8,128)(2,1)}, u32[]{:S(2)}, u32[]{:S(2)}) collective-permute-start(bf16[3,1024,128]{2,1,0:T(8,128)(2,1)} %get-tuple-element.10), channel_id=1, source_target_pairs={{0,8},{8,16},{16,24},{24,32},{32,40},{40,48},{48,56},{56,64},{64,7... | collective-permute-start | bytes 2359304 | tf_op jit(solution)/shard_map/ppermute | solution.py:417
  7.6 1.3 collective-permute-start.1
  8.9 2.5 %inner_rows.1.refs_13_ = bf16[32,8,32,128]{3,2,1,0:T(8,128)(2,1)} custom-call(s32[32,64]{1,0:T(8,128)} %refs_0_.5, bf16[16,1024,128]{2,1,0:T(8,128)(2,1)} %bitcast.17, bf16[7,7,128]{2,1,0:T(8,128)(2,1)} %refs_4_.3, f32[1,128]{1,0:T(1,128)} %bitcast.23, f32[1,128]{1,0:T(1,128)} %bitcast.26, f32[1,128]{1,0:T(1,128)} %bitcast.29, bf16[128,512]{1,0:T(8,128)(2,1)} %refs_8_.5, ...), custom_call_target="tpu_custom_call" | custom-call | flops 9000976384 | bytes 5242880 | tf_op jit(solution)/shard_map/inner_rows/pallas_call | solution.py:303
  11.4 11.8 %collective-permute-done.refs_2_ = bf16[3,1024,128]{2,1,0:T(8,128)(2,1)} collective-permute-done((bf16[3,1024,128]{2,1,0:T(8,128)(2,1)}, bf16[3,1024,128]{2,1,0:T(8,128)(2,1)}, u32[]{:S(2)}, u32[]{:S(2)}) %collective-permute-start) | collective-permute-done | bytes 786464 | tf_op jit(solution)/shard_map/ppermute | solution.py:417
  23.2 4.5 %collective-permute-done.1.refs_3_ = bf16[3,1024,128]{2,1,0:T(8,128)(2,1)} collective-permute-done((bf16[3,1024,128]{2,1,0:T(8,128)(2,1)S(1)}, bf16[3,1024,128]{2,1,0:T(8,128)(2,1)}, u32[]{:S(2)}, u32[]{:S(2)}) %collective-permute-start.1) | collective-permute-done | bytes 786464 | tf_op jit(solution)/shard_map/ppermute | solution.py:418
  27.7 2.9 %edge_rows.1.refs_13_ = bf16[32,8,32,128]{3,2,1,0:T(8,128)(2,1)} custom-call(s32[32,64]{1,0:T(8,128)} %refs_0_.5, bf16[16,1024,128]{2,1,0:T(8,128)(2,1)} %bitcast.18, bf16[3,1024,128]{2,1,0:T(8,128)(2,1)} %collective-permute-done.refs_2_, bf16[3,1024,128]{2,1,0:T(8,128)(2,1)} %collective-permute-done.1.refs_3_, ...), custom_call_target="tpu_custom_call", output_to_operand_aliasing={{}: (13, {})} | custom-call | flops 9000976384 | bytes 5242880 | tf_op jit(solution)/shard_map/edge_rows/pallas_call | solution.py:303
  30.5 21.3 %all-to-all-start = ((bf16[256,32,128]{2,1,0:T(8,128)(2,1)}), bf16[256,32,128]{2,1,0:T(8,128)(2,1)}, u32[]{:S(2)}, u32[]{:S(2)}) async-start(bf16[256,32,128]{2,1,0:T(8,128)(2,1)} %bitcast.16), calls=%async_computation | async-start | bytes 4194304 | tf_op jit(solution)/shard_map/all_to_all | solution.py:425
  51.9 25.5 %full_rows.1 = bf16[32,8,32,128]{3,2,1,0:T(8,128)(2,1)} custom-call(s32[32,64]{1,0:T(8,128)} %refs_0_.5, bf16[16,1024,128]{2,1,0:T(8,128)(2,1)} %bitcast.19, bf16[3,1024,128]{2,1,0:T(8,128)(2,1)} %collective-permute-done.refs_2_, bf16[3,1024,128]{2,1,0:T(8,128)(2,1)} %collective-permute-done.1.refs_3_, bf16[7,7,128]{2,1,0:T(8,128)(2,1)} %refs_4_.3, ...), custom_call_target="tpu_custom_call" | custom-call | flops 18001952768 | bytes 6291456 | tf_op jit(solution)/shard_map/full_rows/pallas_call | solution.py:303
  77.4 27.0 %all-to-all-done = bf16[256,32,128]{2,1,0:T(8,128)(2,1)} async-done(((bf16[256,32,128]{2,1,0:T(8,128)(2,1)}), bf16[256,32,128]{2,1,0:T(8,128)(2,1)}, u32[]{:S(2)}, u32[]{:S(2)}) %all-to-all-start) | async-done | bytes 2097184 | tf_op jit(solution)/shard_map/all_to_all | solution.py:425
  104.4 0.0 copy-start
  104.4 7.5 %all-to-all-start.1 = ((bf16[256,32,128]{2,1,0:T(8,128)(2,1)}), bf16[256,32,128]{2,1,0:T(8,128)(2,1)}, u32[]{:S(2)}, u32[]{:S(2)}) async-start(bf16[256,32,128]{2,1,0:T(8,128)(2,1)} %bitcast.15), calls=%async_computation.1 | async-start | bytes 4194304 | tf_op jit(solution)/shard_map/all_to_all | solution.py:425
  111.9 0.0 copy-done
  111.9 0.1 eq.23
  112.0 0.2 reduce_window_sum.11
  112.2 0.1 subtract_add_fusion
  112.3 0.1 broadcast_in_dim.18
  112.4 0.2 select_reduce_fusion
  112.6 0.6 and_select_fusion
  113.2 51.3 %all-to-all-done.1 = bf16[256,32,128]{2,1,0:T(8,128)(2,1)} async-done(((bf16[256,32,128]{2,1,0:T(8,128)(2,1)}), bf16[256,32,128]{2,1,0:T(8,128)(2,1)}, u32[]{:S(2)}, u32[]{:S(2)}) %all-to-all-start.1) | async-done | bytes 2097184 | tf_op jit(solution)/shard_map/all_to_all | solution.py:425
  164.6 6.1 %vertical.1 = bf16[32,8,32,128]{3,2,1,0:T(8,128)(2,1)} custom-call(s32[32]{0:T(128)} %get-tuple-element.12.src, s32[32]{0:T(128)} %get-tuple-element.11.rank, bf16[32,8,32,128]{3,2,1,0:T(8,128)(2,1)} %bitcast.12.recv0, bf16[32,8,32,128]{3,2,1,0:T(8,128)(2,1)} %bitcast.10.recv1, bf16[5,128,128]{2,1,0:T(8,128)(2,1)} %w_hbm.1), custom_call_target="tpu_custom_call" | custom-call | tf_op jit(solution)/shard_map/vertical/pallas_call | solution.py:391
  (3 shorter events, 0.0 us)
Async XLA Ops:
  2.4 20.9 %collective-permute-start = (bf16[3,1024,128]{2,1,0:T(8,128)(2,1)}, bf16[3,1024,128]{2,1,0:T(8,128)(2,1)}, u32[]{:S(2)}, u32[]{:S(2)}) collective-permute-start(bf16[3,1024,128]{2,1,0:T(8,128)(2,1)} %get-tuple-element.10), channel_id=1, source_target_pairs={{0,8},{8,16},{16,24},{24,32},{32,40},{40,48},{48,56},{56,64},{64,7... | collective-permute-start | bytes 2359304 | tf_op jit(solution)/shard_map/ppermute | solution.py:417
  7.6 20.1 %collective-permute-start.1 = (bf16[3,1024,128]{2,1,0:T(8,128)(2,1)S(1)}, bf16[3,1024,128]{2,1,0:T(8,128)(2,1)}, u32[]{:S(2)}, u32[]{:S(2)}) collective-permute-start(bf16[3,1024,128]{2,1,0:T(8,128)(2,1)S(1)} %get-tuple-element.9), channel_id=1, source_target_pairs={{8,0},{16,8},{24,16},{32,24},{40,32},{48,40},{56,48},{64,56},{72,6... | collective-permute-start | bytes 2359304 | tf_op jit(solution)/shard_map/ppermute | solution.py:418
  30.5 73.8 %all-to-all-start = ((bf16[256,32,128]{2,1,0:T(8,128)(2,1)}), bf16[256,32,128]{2,1,0:T(8,128)(2,1)}, u32[]{:S(2)}, u32[]{:S(2)}) async-start(bf16[256,32,128]{2,1,0:T(8,128)(2,1)} %bitcast.16), calls=%async_computation | async-start | bytes 4194304 | tf_op jit(solution)/shard_map/all_to_all | solution.py:425
  104.4 7.6 %copy-start = (s32[32,64]{1,0:T(8,128)S(1)}, s32[32,64]{1,0:T(8,128)}, u32[]{:S(2)}) copy-start(s32[32,64]{1,0:T(8,128)} %refs_0_.5) | copy-start | bytes 24580
  104.4 60.2 %all-to-all-start.1 = ((bf16[256,32,128]{2,1,0:T(8,128)(2,1)}), bf16[256,32,128]{2,1,0:T(8,128)(2,1)}, u32[]{:S(2)}, u32[]{:S(2)}) async-start(bf16[256,32,128]{2,1,0:T(8,128)(2,1)} %bitcast.15), calls=%async_computation.1 | async-start | bytes 4194304 | tf_op jit(solution)/shard_map/all_to_all | solution.py:425

commit v4 on v3

--- a/solution.py
+++ b/solution.py
@@ -326,7 +326,7 @@
     )(*args, *passed)
 
 
-GROUP = 4
+GROUP = 8
 
 
 def vertical_kernel(src, rank, recv0, recv1, w_hbm, out, held, done, taps, w, sem_in,
@@ -348,7 +348,7 @@
 
     weights = pltpu.make_async_copy(w_hbm, taps, sem_w)
     weights.start()
-    lax.fori_loop(0, tiles, start, 0)
+    lax.fori_loop(0, tiles, start, 0, unroll=8)
     weights.wait()
     for d in range(6):
         for p in range(2):
@@ -407,6 +407,36 @@
     )(src, rank, recv0, recv1, w_vert)
 
 
+def halo_kernel(x, first, last, held, sem):
+    rows = first.shape[0]
+    ends = [(0, first), (x.shape[0] - rows, last)]
+    loads = [pltpu.make_async_copy(x.at[pl.ds(row, rows)], held.at[q], sem.at[q])
+             for q, (row, _) in enumerate(ends)]
+    stores = [pltpu.make_async_copy(held.at[q], out, sem.at[2 + q])
+              for q, (_, out) in enumerate(ends)]
+    for cp in loads:
+        cp.start()
+    for load, store in zip(loads, stores):
+        load.wait()
+        store.start()
+    for cp in stores:
+        cp.wait()
+
+
+def halo_call(x, rows):
+    hbm = pl.BlockSpec(memory_space=pltpu.HBM)
+    shape = jax.ShapeDtypeStruct((rows,) + x.shape[1:], x.dtype)
+    return pl.pallas_call(
+        halo_kernel,
+        in_specs=[hbm],
+        out_specs=[hbm] * 2,
+        out_shape=[shape] * 2,
+        scratch_shapes=[pltpu.VMEM((2, rows) + x.shape[1:], x.dtype), pltpu.SemaphoreType.DMA((4,))],
+        compiler_params=pltpu.CompilerParams(vmem_limit_bytes=VMEM_BYTES),
+        name="halo_rows",
+    )(x)
+
+
 def body(ocean_state, tile_owner, kernel, bias_dw, ln_gain, ln_bias, w_in, b_in, w_out, b_out,
          layer_scale, w_vert):
     bands, lon = tile_owner.shape
@@ -414,8 +444,9 @@
     band = lax.axis_index("tile")
     x = ocean_state[0]
     ends = bands - 1
-    top = lax.ppermute(x[TS - 3 :], "tile", [(i, i + 1) for i in range(ends)])
-    bottom = lax.ppermute(x[:3], "tile", [(i + 1, i) for i in range(ends)])
+    head, tail = halo_call(x, 3)
+    top = lax.ppermute(tail, "tile", [(i, i + 1) for i in range(ends)])
+    bottom = lax.ppermute(head, "tile", [(i + 1, i) for i in range(ends)])
     row = lambda v: v.reshape(1, -1)
     consts = (kernel, row(bias_dw), row(ln_gain), row(ln_bias), w_in, row(b_in), w_out, row(b_out),
               row(layer_scale))

time: 170 us -> 173 us (1.018)
  local copies, waits for them, and re-layouts: 2.51 us -> 0.15 us
  starting transfers between devices: 35.4 us -> 37.7 us
  Pallas kernels: 37 us -> 38.8 us
    all_to_all x2, starting transfers between devices: 28.8 us -> 32 us  [exchange(): lax.all_to_all(sent.reshape((bands * levels,) + sent.shape[2:]), ('tile',...]
    slice x1 -> x0, local copies, waits for them, and re-layouts: 2.36 us -> none  [body(): bottom = lax.ppermute(x[:3], 'tile', [(i + 1, i) for i in range(ends)])]
    pallas_call x0 -> x1, Pallas kernels: none -> 2.33 us  [halo_call(): pl.pallas_call(halo_kernel, in_specs=[hbm], out_specs=[hbm] * 2, out_shap...]
where the time goes in v4:
time: 173 us
  waiting for transfers between devices  95 us (55%)
  Pallas kernels  38.8 us (22%)
  starting transfers between devices  37.7 us (22%)
    all_to_all x2, waiting for transfers between devices, exchange(): lax.all_to_all(sent.reshape((bands * levels,) + sent.shape[2:]), ('tile',...  78.3 us
    all_to_all x2, starting transfers between devices, exchange(): lax.all_to_all(sent.reshape((bands * levels,) + sent.shape[2:]), ('tile',...  32 us
    pallas_call x3, Pallas kernels, block_call(): pl.pallas_call(functools.partial(block_kernel, rows, want, batch, n_args,...  30.9 us
    ppermute x1, waiting for transfers between devices, body(): top = lax.ppermute(tail, 'tile', [(i, i + 1) for i in range(ends)])  12.6 us
    pallas_call x1, Pallas kernels, vertical_call(): pl.pallas_call(vertical_kernel, in_specs=[smem, smem, hbm, hbm, hbm], out...  5.53 us
    ppermute x1, starting transfers between devices, body(): top = lax.ppermute(tail, 'tile', [(i, i + 1) for i in range(ends)])  4.42 us
    ppermute x1, waiting for transfers between devices, body(): bottom = lax.ppermute(head, 'tile', [(i + 1, i) for i in range(ends)])  4.13 us
  transfers between devices with their start and end apart: 4, of which 4 were waited for; matrix products, arithmetic and copies ran while one was open for 1% of the time, Pallas kernels for 16%

profile of v4, /device:TPU:1, one launch (start us, length us, event | category | flops | bytes accessed | tf_op | source)
XLA Modules:
  0.0 173.0 jit_solution(17744080511299875543)
XLA Ops:
  0.0 2.3 %halo_rows.1 = (bf16[3,1024,128]{2,1,0:T(8,128)(2,1)}, bf16[3,1024,128]{2,1,0:T(8,128)(2,1)}) custom-call(bf16[16,1024,128]{2,1,0:T(8,128)(2,1)} %bitcast.11), custom_call_target="tpu_custom_call" | custom-call | tf_op jit(solution)/shard_map/halo_rows/pallas_call | solution.py:429
  2.3 4.4 %collective-permute-start = (bf16[3,1024,128]{2,1,0:T(8,128)(2,1)}, bf16[3,1024,128]{2,1,0:T(8,128)(2,1)S(1)}, u32[]{:S(2)}, u32[]{:S(2)}) collective-permute-start(bf16[3,1024,128]{2,1,0:T(8,128)(2,1)} %get-tuple-element.9), channel_id=1, source_target_pairs={{0,8},{8,16},{16,24},{24,32},{32,40},{40,48},{48,56},{56,64},{64,7... | collective-permute-start | bytes 2359304 | tf_op jit(solution)/shard_map/ppermute | solution.py:448
  6.8 1.3 collective-permute-start.1
  8.1 2.5 %inner_rows.1.refs_13_ = bf16[32,8,32,128]{3,2,1,0:T(8,128)(2,1)} custom-call(s32[32,64]{1,0:T(8,128)} %refs_0_.5, bf16[16,1024,128]{2,1,0:T(8,128)(2,1)} %bitcast.12, bf16[7,7,128]{2,1,0:T(8,128)(2,1)} %refs_4_.3, f32[1,128]{1,0:T(1,128)} %bitcast.20, f32[1,128]{1,0:T(1,128)} %bitcast.23, f32[1,128]{1,0:T(1,128)} %bitcast.26, bf16[128,512]{1,0:T(8,128)(2,1)} %refs_8_.5, ...), custom_call_target="tpu_custom_call" | custom-call | flops 9000976384 | bytes 5242880 | tf_op jit(solution)/shard_map/inner_rows/pallas_call | solution.py:303
  10.6 12.6 %collective-permute-done.refs_2_ = bf16[3,1024,128]{2,1,0:T(8,128)(2,1)S(1)} collective-permute-done((bf16[3,1024,128]{2,1,0:T(8,128)(2,1)}, bf16[3,1024,128]{2,1,0:T(8,128)(2,1)S(1)}, u32[]{:S(2)}, u32[]{:S(2)}) %collective-permute-start) | collective-permute-done | bytes 786464 | tf_op jit(solution)/shard_map/ppermute | solution.py:448
  23.2 0.0 copy-start.1
  23.2 4.1 %collective-permute-done.1.refs_3_ = bf16[3,1024,128]{2,1,0:T(8,128)(2,1)} collective-permute-done((bf16[3,1024,128]{2,1,0:T(8,128)(2,1)}, bf16[3,1024,128]{2,1,0:T(8,128)(2,1)}, u32[]{:S(2)}, u32[]{:S(2)}) %collective-permute-start.1) | collective-permute-done | bytes 786464 | tf_op jit(solution)/shard_map/ppermute | solution.py:449
  27.4 0.0 copy-done.1
  27.4 2.9 %edge_rows.1.refs_13_ = bf16[32,8,32,128]{3,2,1,0:T(8,128)(2,1)} custom-call(s32[32,64]{1,0:T(8,128)} %refs_0_.5, bf16[16,1024,128]{2,1,0:T(8,128)(2,1)} %bitcast.13, bf16[3,1024,128]{2,1,0:T(8,128)(2,1)} %copy-done.1, bf16[3,1024,128]{2,1,0:T(8,128)(2,1)} %collective-permute-done.1.refs_3_, ...), custom_call_target="tpu_custom_call", output_to_operand_aliasing={{}: (13, {})} | custom-call | flops 9000976384 | bytes 5242880 | tf_op jit(solution)/shard_map/edge_rows/pallas_call | solution.py:303
  30.2 24.5 %all-to-all-start = ((bf16[256,32,128]{2,1,0:T(8,128)(2,1)}), bf16[256,32,128]{2,1,0:T(8,128)(2,1)}, u32[]{:S(2)}, u32[]{:S(2)}) async-start(bf16[256,32,128]{2,1,0:T(8,128)(2,1)} %bitcast.16), calls=%async_computation | async-start | bytes 4194304 | tf_op jit(solution)/shard_map/all_to_all | solution.py:456
  54.7 25.5 %full_rows.1 = bf16[32,8,32,128]{3,2,1,0:T(8,128)(2,1)} custom-call(s32[32,64]{1,0:T(8,128)} %refs_0_.5, bf16[16,1024,128]{2,1,0:T(8,128)(2,1)} %bitcast.14, bf16[3,1024,128]{2,1,0:T(8,128)(2,1)} %copy-done.1, bf16[3,1024,128]{2,1,0:T(8,128)(2,1)} %collective-permute-done.1.refs_3_, bf16[7,7,128]{2,1,0:T(8,128)(2,1)} %refs_4_.3, f32[1,128]{1,0:T(1,128)} %bitcast.22, ...), custom_call_target="tpu_custom_call" | custom-call | flops 18001952768 | bytes 6291456 | tf_op jit(solution)/shard_map/full_rows/pallas_call | solution.py:303
  80.3 27.0 %all-to-all-done = bf16[256,32,128]{2,1,0:T(8,128)(2,1)} async-done(((bf16[256,32,128]{2,1,0:T(8,128)(2,1)}), bf16[256,32,128]{2,1,0:T(8,128)(2,1)}, u32[]{:S(2)}, u32[]{:S(2)}) %all-to-all-start) | async-done | bytes 2097184 | tf_op jit(solution)/shard_map/all_to_all | solution.py:456
  107.2 0.0 copy-start
  107.2 7.5 %all-to-all-start.1 = ((bf16[256,32,128]{2,1,0:T(8,128)(2,1)}), bf16[256,32,128]{2,1,0:T(8,128)(2,1)}, u32[]{:S(2)}, u32[]{:S(2)}) async-start(bf16[256,32,128]{2,1,0:T(8,128)(2,1)} %bitcast.15), calls=%async_computation.1 | async-start | bytes 4194304 | tf_op jit(solution)/shard_map/all_to_all | solution.py:456
  114.8 0.0 copy-done
  114.8 0.1 eq.23
  114.9 0.2 reduce_window_sum.11
  115.1 0.1 subtract_add_fusion
  115.2 0.1 broadcast_in_dim.18
  115.3 0.2 select_reduce_fusion
  115.5 0.6 and_select_fusion
  116.1 51.3 %all-to-all-done.1 = bf16[256,32,128]{2,1,0:T(8,128)(2,1)} async-done(((bf16[256,32,128]{2,1,0:T(8,128)(2,1)}), bf16[256,32,128]{2,1,0:T(8,128)(2,1)}, u32[]{:S(2)}, u32[]{:S(2)}) %all-to-all-start.1) | async-done | bytes 2097184 | tf_op jit(solution)/shard_map/all_to_all | solution.py:456
  167.4 5.5 %vertical.1 = bf16[32,8,32,128]{3,2,1,0:T(8,128)(2,1)} custom-call(s32[32]{0:T(128)} %get-tuple-element.14.src, s32[32]{0:T(128)} %get-tuple-element.13.rank, bf16[32,8,32,128]{3,2,1,0:T(8,128)(2,1)} %bitcast.10.recv0, bf16[32,8,32,128]{3,2,1,0:T(8,128)(2,1)} %bitcast.8.recv1, bf16[5,128,128]{2,1,0:T(8,128)(2,1)} %w_hbm.1), custom_call_target="tpu_custom_call" | custom-call | tf_op jit(solution)/shard_map/vertical/pallas_call | solution.py:391
  (3 shorter events, 0.0 us)
Async XLA Ops:
  2.3 20.9 %collective-permute-start = (bf16[3,1024,128]{2,1,0:T(8,128)(2,1)}, bf16[3,1024,128]{2,1,0:T(8,128)(2,1)S(1)}, u32[]{:S(2)}, u32[]{:S(2)}) collective-permute-start(bf16[3,1024,128]{2,1,0:T(8,128)(2,1)} %get-tuple-element.9), channel_id=1, source_target_pairs={{0,8},{8,16},{16,24},{24,32},{32,40},{40,48},{48,56},{56,64},{64,7... | collective-permute-start | bytes 2359304 | tf_op jit(solution)/shard_map/ppermute | solution.py:448
  6.8 20.6 %collective-permute-start.1 = (bf16[3,1024,128]{2,1,0:T(8,128)(2,1)}, bf16[3,1024,128]{2,1,0:T(8,128)(2,1)}, u32[]{:S(2)}, u32[]{:S(2)}) collective-permute-start(bf16[3,1024,128]{2,1,0:T(8,128)(2,1)} %get-tuple-element.10), channel_id=1, source_target_pairs={{8,0},{16,8},{24,16},{32,24},{40,32},{48,40},{56,48},{64,56},{72,6... | collective-permute-start | bytes 2359304 | tf_op jit(solution)/shard_map/ppermute | solution.py:449
  23.2 4.1 %copy-start.1 = (bf16[3,1024,128]{2,1,0:T(8,128)(2,1)}, bf16[3,1024,128]{2,1,0:T(8,128)(2,1)S(1)}, u32[]{:S(2)}) copy-start(bf16[3,1024,128]{2,1,0:T(8,128)(2,1)S(1)} %collective-permute-done.refs_2_) | copy-start | bytes 2359300
  30.2 77.0 %all-to-all-start = ((bf16[256,32,128]{2,1,0:T(8,128)(2,1)}), bf16[256,32,128]{2,1,0:T(8,128)(2,1)}, u32[]{:S(2)}, u32[]{:S(2)}) async-start(bf16[256,32,128]{2,1,0:T(8,128)(2,1)} %bitcast.16), calls=%async_computation | async-start | bytes 4194304 | tf_op jit(solution)/shard_map/all_to_all | solution.py:456
  107.2 7.6 %copy-start = (s32[32,64]{1,0:T(8,128)S(1)}, s32[32,64]{1,0:T(8,128)}, u32[]{:S(2)}) copy-start(s32[32,64]{1,0:T(8,128)} %refs_0_.5) | copy-start | bytes 24580
  107.2 60.2 %all-to-all-start.1 = ((bf16[256,32,128]{2,1,0:T(8,128)(2,1)}), bf16[256,32,128]{2,1,0:T(8,128)(2,1)}, u32[]{:S(2)}, u32[]{:S(2)}) async-start(bf16[256,32,128]{2,1,0:T(8,128)(2,1)} %bitcast.15), calls=%async_computation.1 | async-start | bytes 4194304 | tf_op jit(solution)/shard_map/all_to_all | solution.py:456

commit v5 on v4

--- a/solution.py
+++ b/solution.py
@@ -159,8 +159,8 @@
     return (owner_ref[band, left] >= 0, owner_ref[band, t] >= 0, owner_ref[band, right] >= 0)
 
 
-INNER, EDGES, FULL = "inner_rows", "edge_rows", "full_rows"
-CELLS = {INNER: 128, EDGES: 128, FULL: 256}
+INNER, UPPER, LOWER, FULL = "inner_rows", "upper_rows", "lower_rows", "full_rows"
+CELLS = {INNER: 128, UPPER: 64, LOWER: 64, FULL: 256}
 
 
 def block_kernel(rows, want, batch, n_args, n_pass, *refs):
@@ -170,16 +170,15 @@
     wide, taps, convbuf, inbuf, stage, seen, cols, dests, sem, load = refs
     loads = []
     for q, (src, dst) in enumerate(zip(args, held)):
-        if rows == EDGES and q == 1:
-            loads.append(pltpu.make_async_copy(src.at[pl.ds(0, 7)], dst.at[pl.ds(0, 7)], load.at[q]))
-            loads.append(pltpu.make_async_copy(src.at[pl.ds(9, 7)], dst.at[pl.ds(7, 7)], load.at[n_args]))
+        if rows in (UPPER, LOWER) and q == 1:
+            part = src.at[pl.ds(0 if rows == UPPER else 9, 7)]
+            loads.append(pltpu.make_async_copy(part, dst, load.at[q]))
         else:
             loads.append(pltpu.make_async_copy(src, dst, load.at[q]))
     for cp in loads:
         cp.start()
     owner_ref, x_ref = held[:2]
-    if rows != INNER:
-        top, bottom = held[2:4]
+    top, bottom = held[2], held[-10]
     taps_in, bias_ref, gain, shift, w_in, b_in, w_out, b_out, scale = held[-9:]
     bands, lon = owner_ref.shape
     band = lax.axis_index("tile")
@@ -207,7 +206,7 @@
             return [piece(0, 0, 2 * half, 0)]
         if rows == INNER:
             return [piece(0, 0, half, half // 2)]
-        return [piece(0, 0, half // 2, 0), piece(1, half // 2, half // 2, half + half // 2)]
+        return [piece(0, 0, half // 2, 0 if rows == UPPER else half + half // 2)]
 
     def each_copy(k, b, act):
         for q in range(batch):
@@ -246,10 +245,12 @@
             cut = window(x_ref, range(1, 15))
             put(0, [cut[:10], cut[4:]])
             inbuf[q] = x_ref[pl.ds(4, 8), column, :].reshape(cells, C)
-        elif rows == EDGES:
-            put(0, [above(7), below(7)])
-            inbuf[q, pl.ds(0, 64)] = x_ref[pl.ds(0, 4), column, :].reshape(64, C)
-            inbuf[q, pl.ds(64, 64)] = x_ref[pl.ds(10, 4), column, :].reshape(64, C)
+        elif rows == UPPER:
+            put(0, [above(7)])
+            inbuf[q] = x_ref[pl.ds(0, 4), column, :].reshape(cells, C)
+        elif rows == LOWER:
+            put(0, [below(7)])
+            inbuf[q] = x_ref[pl.ds(3, 4), column, :].reshape(cells, C)
         else:
             cut = above(11)
             put(0, [cut[:10], cut[4:]])
@@ -295,7 +296,7 @@
     args = [owner, x, *halos, *consts]
     n_args = len(args)
     held = [pltpu.SMEM(owner.shape, owner.dtype)]
-    held.append(pltpu.VMEM((14 if rows == EDGES else x.shape[0],) + x.shape[1:], x.dtype))
+    held.append(pltpu.VMEM((7 if rows in (UPPER, LOWER) else x.shape[0],) + x.shape[1:], x.dtype))
     held += [pltpu.VMEM(v.shape, v.dtype) for v in args[2:]]
     passed = [v for v in (alias, after) if v is not None]
     cells = CELLS[rows]
@@ -459,7 +460,8 @@
         ).reshape(sent.shape)
 
     sent1 = block_call(INNER, 1, 4, tile_owner, x, (), consts, levels)
-    sent1 = block_call(EDGES, 1, 4, tile_owner, x, halos, consts, levels, alias=sent1)
+    sent1 = block_call(UPPER, 1, 8, tile_owner, x, (top,), consts, levels, alias=sent1)
+    sent1 = block_call(LOWER, 1, 8, tile_owner, x, (bottom,), consts, levels, alias=sent1)
     sent0 = block_call(FULL, 0, 4, tile_owner, x, halos, consts, levels, after=sent1)
     sent0, recv1 = lax.optimization_barrier((sent0, exchange(sent1)))
     recv0 = exchange(sent0)

time: 173 us -> 176 us (1.017)
  starting transfers between devices: 37.7 us -> 41.1 us
  waiting for transfers between devices: 95 us -> 91.9 us
    all_to_all x2, starting transfers between devices: 32 us -> 35.4 us  [exchange(): lax.all_to_all(sent.reshape((bands * levels,) + sent.shape[2:]), ('tile',...]
    ppermute x1, waiting for transfers between devices: 4.13 us -> 0.98 us  [body(): bottom = lax.ppermute(head, 'tile', [(i + 1, i) for i in range(ends)])]
    pallas_call x3 -> x4, Pallas kernels: 30.9 us -> 32.6 us  [block_call(): pl.pallas_call(functools.partial(block_kernel, rows, want, batch, n_args,...]
  transfers between devices with their start and end apart: 4 -> 4, of which waited for: 4 -> 4; matrix products, arithmetic and copies ran while one was open for 1% -> 1% of each run, Pallas kernels for 16% -> 17%
where the time goes in v5:
time: 176 us
  waiting for transfers between devices  91.9 us (52%)
  starting transfers between devices  41.1 us (23%)
  Pallas kernels  40.5 us (23%)
    all_to_all x2, waiting for transfers between devices, exchange(): lax.all_to_all(sent.reshape((bands * levels,) + sent.shape[2:]), ('tile',...  78.3 us
    all_to_all x2, starting transfers between devices, exchange(): lax.all_to_all(sent.reshape((bands * levels,) + sent.shape[2:]), ('tile',...  35.4 us
    pallas_call x4, Pallas kernels, block_call(): pl.pallas_call(functools.partial(block_kernel, rows, want, batch, n_args,...  32.6 us
    ppermute x1, waiting for transfers between devices, body(): top = lax.ppermute(tail, 'tile', [(i, i + 1) for i in range(ends)])  12.6 us
    pallas_call x1, Pallas kernels, vertical_call(): pl.pallas_call(vertical_kernel, in_specs=[smem, smem, hbm, hbm, hbm], out...  5.53 us
    ppermute x1, starting transfers between devices, body(): top = lax.ppermute(tail, 'tile', [(i, i + 1) for i in range(ends)])  4.42 us
  transfers between devices with their start and end apart: 4, of which 4 were waited for; matrix products, arithmetic and copies ran while one was open for 1% of the time, Pallas kernels for 17%

profile of v5, /device:TPU:1, one launch (start us, length us, event | category | flops | bytes accessed | tf_op | source)
XLA Modules:
  0.0 175.7 jit_solution(5590761699349329818)
XLA Ops:
  0.0 2.3 %halo_rows.1 = (bf16[3,1024,128]{2,1,0:T(8,128)(2,1)}, bf16[3,1024,128]{2,1,0:T(8,128)(2,1)}) custom-call(bf16[16,1024,128]{2,1,0:T(8,128)(2,1)} %bitcast.11), custom_call_target="tpu_custom_call" | custom-call | tf_op jit(solution)/shard_map/halo_rows/pallas_call | solution.py:430
  2.3 4.4 %collective-permute-start = (bf16[3,1024,128]{2,1,0:T(8,128)(2,1)}, bf16[3,1024,128]{2,1,0:T(8,128)(2,1)S(1)}, u32[]{:S(2)}, u32[]{:S(2)}) collective-permute-start(bf16[3,1024,128]{2,1,0:T(8,128)(2,1)} %get-tuple-element.9), channel_id=1, source_target_pairs={{0,8},{8,16},{16,24},{24,32},{32,40},{40,48},{48,56},{56,64},{64,7... | collective-permute-start | bytes 2359304 | tf_op jit(solution)/shard_map/ppermute | solution.py:449
  6.8 1.3 collective-permute-start.1
  8.1 2.5 %inner_rows.1.refs_12_ = bf16[32,8,32,128]{3,2,1,0:T(8,128)(2,1)} custom-call(s32[32,64]{1,0:T(8,128)} %refs_0_.7, bf16[16,1024,128]{2,1,0:T(8,128)(2,1)} %bitcast.12, bf16[7,7,128]{2,1,0:T(8,128)(2,1)} %refs_4_.1, f32[1,128]{1,0:T(1,128)} %bitcast.22, f32[1,128]{1,0:T(1,128)} %bitcast.26, f32[1,128]{1,0:T(1,128)} %bitcast.30, bf16[128,512]{1,0:T(8,128)(2,1)} %refs_8_.3, ...), custom_call_target="tpu_custom_call" | custom-call | flops 9000976384 | bytes 5242880 | tf_op jit(solution)/shard_map/inner_rows/pallas_call | solution.py:304
  10.6 12.6 %collective-permute-done.refs_2_ = bf16[3,1024,128]{2,1,0:T(8,128)(2,1)S(1)} collective-permute-done((bf16[3,1024,128]{2,1,0:T(8,128)(2,1)}, bf16[3,1024,128]{2,1,0:T(8,128)(2,1)S(1)}, u32[]{:S(2)}, u32[]{:S(2)}) %collective-permute-start) | collective-permute-done | bytes 786464 | tf_op jit(solution)/shard_map/ppermute | solution.py:449
  23.2 0.0 copy-start.1
  23.2 0.9 copy-done.1
  24.1 2.3 %upper_rows.1.refs_12_ = bf16[32,8,32,128]{3,2,1,0:T(8,128)(2,1)} custom-call(s32[32,64]{1,0:T(8,128)} %refs_0_.7, bf16[16,1024,128]{2,1,0:T(8,128)(2,1)} %bitcast.13, bf16[3,1024,128]{2,1,0:T(8,128)(2,1)} %copy-done.1, bf16[7,7,128]{2,1,0:T(8,128)(2,1)} %refs_4_.1, f32[1,128]{1,0:T(1,128)} %bitcast.23, ...), custom_call_target="tpu_custom_call", output_to_operand_aliasing={{}: (12, {})} | custom-call | flops 4500488192 | bytes 4718592 | tf_op jit(solution)/shard_map/upper_rows/pallas_call | solution.py:304
  26.4 1.0 collective-permute-done.1.refs_2_.refs_3_
  27.4 2.3 %lower_rows.1.refs_13_ = bf16[32,8,32,128]{3,2,1,0:T(8,128)(2,1)} custom-call(s32[32,64]{1,0:T(8,128)} %refs_0_.7, bf16[16,1024,128]{2,1,0:T(8,128)(2,1)} %bitcast.14, bf16[3,1024,128]{2,1,0:T(8,128)(2,1)} %collective-permute-done.1.refs_2_.refs_3_, bf16[7,7,128]{2,1,0:T(8,128)(2,1)} %refs_4_.1, f32[1,128]{1,0:T(1,128)} %bitcast.24, ...), custom_call_target="tpu_custom_call", output_to_operand_aliasing={{}: (12, {})} | custom-call | flops 4500488192 | bytes 4718592 | tf_op jit(solution)/shard_map/lower_rows/pallas_call | solution.py:304
  29.6 27.8 %all-to-all-start = ((bf16[256,32,128]{2,1,0:T(8,128)(2,1)}), bf16[256,32,128]{2,1,0:T(8,128)(2,1)}, u32[]{:S(2)}, u32[]{:S(2)}) async-start(bf16[256,32,128]{2,1,0:T(8,128)(2,1)} %bitcast.17), calls=%async_computation | async-start | bytes 4194304 | tf_op jit(solution)/shard_map/all_to_all | solution.py:457
  57.5 25.6 %full_rows.1 = bf16[32,8,32,128]{3,2,1,0:T(8,128)(2,1)} custom-call(s32[32,64]{1,0:T(8,128)} %refs_0_.7, bf16[16,1024,128]{2,1,0:T(8,128)(2,1)} %bitcast.15, bf16[3,1024,128]{2,1,0:T(8,128)(2,1)} %copy-done.1, bf16[3,1024,128]{2,1,0:T(8,128)(2,1)} %collective-permute-done.1.refs_2_.refs_3_, bf16[7,7,128]{2,1,0:T(8,128)(2,1)} %refs_4_.1, f32[1,128]{1,0:T(1,128)} %bitcast.25, ...), custom_call_target="tpu_custom_call" | custom-call | flops 18001952768 | bytes 6291456 | tf_op jit(solution)/shard_map/full_rows/pallas_call | solution.py:304
  83.0 26.9 %all-to-all-done = bf16[256,32,128]{2,1,0:T(8,128)(2,1)} async-done(((bf16[256,32,128]{2,1,0:T(8,128)(2,1)}), bf16[256,32,128]{2,1,0:T(8,128)(2,1)}, u32[]{:S(2)}, u32[]{:S(2)}) %all-to-all-start) | async-done | bytes 2097184 | tf_op jit(solution)/shard_map/all_to_all | solution.py:457
  110.0 0.0 copy-start
  110.0 7.5 %all-to-all-start.1 = ((bf16[256,32,128]{2,1,0:T(8,128)(2,1)}), bf16[256,32,128]{2,1,0:T(8,128)(2,1)}, u32[]{:S(2)}, u32[]{:S(2)}) async-start(bf16[256,32,128]{2,1,0:T(8,128)(2,1)} %bitcast.16), calls=%async_computation.1 | async-start | bytes 4194304 | tf_op jit(solution)/shard_map/all_to_all | solution.py:457
  117.5 0.0 copy-done
  117.5 0.1 eq.23
  117.6 0.2 reduce_window_sum.11
  117.9 0.1 subtract_add_fusion
  117.9 0.1 broadcast_in_dim.18
  118.0 0.2 select_reduce_fusion
  118.2 0.6 and_select_fusion
  118.8 51.3 %all-to-all-done.1 = bf16[256,32,128]{2,1,0:T(8,128)(2,1)} async-done(((bf16[256,32,128]{2,1,0:T(8,128)(2,1)}), bf16[256,32,128]{2,1,0:T(8,128)(2,1)}, u32[]{:S(2)}, u32[]{:S(2)}) %all-to-all-start.1) | async-done | bytes 2097184 | tf_op jit(solution)/shard_map/all_to_all | solution.py:457
  170.2 5.5 %vertical.1 = bf16[32,8,32,128]{3,2,1,0:T(8,128)(2,1)} custom-call(s32[32]{0:T(128)} %get-tuple-element.14.src, s32[32]{0:T(128)} %get-tuple-element.13.rank, bf16[32,8,32,128]{3,2,1,0:T(8,128)(2,1)} %bitcast.10.recv0, bf16[32,8,32,128]{3,2,1,0:T(8,128)(2,1)} %bitcast.8.recv1, bf16[5,128,128]{2,1,0:T(8,128)(2,1)} %w_hbm.1), custom_call_target="tpu_custom_call" | custom-call | tf_op jit(solution)/shard_map/vertical/pallas_call | solution.py:392
  (3 shorter events, 0.0 us)
Async XLA Ops:
  2.3 20.9 %collective-permute-start = (bf16[3,1024,128]{2,1,0:T(8,128)(2,1)}, bf16[3,1024,128]{2,1,0:T(8,128)(2,1)S(1)}, u32[]{:S(2)}, u32[]{:S(2)}) collective-permute-start(bf16[3,1024,128]{2,1,0:T(8,128)(2,1)} %get-tuple-element.9), channel_id=1, source_target_pairs={{0,8},{8,16},{16,24},{24,32},{32,40},{40,48},{48,56},{56,64},{64,7... | collective-permute-start | bytes 2359304 | tf_op jit(solution)/shard_map/ppermute | solution.py:449
  6.8 20.6 %collective-permute-start.1 = (bf16[3,1024,128]{2,1,0:T(8,128)(2,1)}, bf16[3,1024,128]{2,1,0:T(8,128)(2,1)}, u32[]{:S(2)}, u32[]{:S(2)}) collective-permute-start(bf16[3,1024,128]{2,1,0:T(8,128)(2,1)} %get-tuple-element.10), channel_id=1, source_target_pairs={{8,0},{16,8},{24,16},{32,24},{40,32},{48,40},{56,48},{64,56},{72,6... | collective-permute-start | bytes 2359304 | tf_op jit(solution)/shard_map/ppermute | solution.py:450
  23.2 0.9 copy-start.1
  29.6 80.3 %all-to-all-start = ((bf16[256,32,128]{2,1,0:T(8,128)(2,1)}), bf16[256,32,128]{2,1,0:T(8,128)(2,1)}, u32[]{:S(2)}, u32[]{:S(2)}) async-start(bf16[256,32,128]{2,1,0:T(8,128)(2,1)} %bitcast.17), calls=%async_computation | async-start | bytes 4194304 | tf_op jit(solution)/shard_map/all_to_all | solution.py:457
  110.0 7.6 %copy-start = (s32[32,64]{1,0:T(8,128)S(1)}, s32[32,64]{1,0:T(8,128)}, u32[]{:S(2)}) copy-start(s32[32,64]{1,0:T(8,128)} %refs_0_.7) | copy-start | bytes 24580
  110.0 60.2 %all-to-all-start.1 = ((bf16[256,32,128]{2,1,0:T(8,128)(2,1)}), bf16[256,32,128]{2,1,0:T(8,128)(2,1)}, u32[]{:S(2)}, u32[]{:S(2)}) async-start(bf16[256,32,128]{2,1,0:T(8,128)(2,1)} %bitcast.16), calls=%async_computation.1 | async-start | bytes 4194304 | tf_op jit(solution)/shard_map/all_to_all | solution.py:457
